TPU v7x, 32 devices: a whole 2x2x4 slice. The times are simulated.
32 devices in a mesh: shard: 8 (over z, y), replica: 4 (over x, core).
Axes of the slice: x: 2, y: 2, z: 4, core: 2. Of those that a mesh axis runs over, the one named last changes fastest.
Arguments:
- inputs: bfloat16 [2, 4, 2048, 1024], P(None, 'replica', 'shard'), may hold values from -6 to 6
- prefix: int32 [2, 4, 1], P(None, 'replica'), may hold values from 1 to 2048
- qkv_weight: bfloat16 [1024, 3072], P('shard'), may hold values from -0.1875 to 0.1875
- qv_bias: bfloat16 [2, 1024], P(None, 'shard'), may hold values from -3 to 3
- out_weight: bfloat16 [1024, 1024], P('shard'), may hold values from -0.1875 to 0.1875
- branch_bias: bfloat16 [2, 1024], P(None, 'shard'), may hold values from -3 to 3
- up_weight: bfloat16 [1024, 4096], P('shard'), may hold values from -0.1875 to 0.1875
- up_bias: bfloat16 [4096], P('shard'), may hold values from -3 to 3
- down_weight: bfloat16 [4096, 1024], P('shard'), may hold values from -0.09375 to 0.09375
- norm_gain: bfloat16 [4, 1024], P(None, 'shard'), may hold values from 0.5 to 1.5
- norm_bias: bfloat16 [4, 1024], P(None, 'shard'), may hold values from -2 to 2
- cotangent: bfloat16 [2, 4, 2048, 1024], P(None, 'replica', 'shard'), may hold values from -6 to 6
Outputs:
- output: bfloat16 [2, 4, 2048, 1024], P(None, 'replica', 'shard')
- input_grad: bfloat16 [2, 4, 2048, 1024], P(None, 'replica', 'shard')
- grad_qkv_weight: float32 [1024, 3072], P('shard')
- grad_qv_bias: float32 [2, 1024], P(None, 'shard')
- grad_out_weight: float32 [1024, 1024], P('shard')
- grad_branch_bias: float32 [2, 1024], P(None, 'shard')
- grad_up_weight: float32 [1024, 4096], P('shard')
- grad_up_bias: float32 [4096], P('shard')
- grad_down_weight: float32 [4096, 1024], P('shard')
- grad_norm_gain: float32 [4, 1024], P(None, 'shard')
- grad_norm_bias: float32 [4, 1024], P(None, 'shard')
Inputs may be any that keep to these rules, and one draw needn't show every extreme that they name: Each sequence's first prefix positions are seen by all of its positions.
All inputs are finite; a program needn't handle non-finite values.
Results may differ from a plain program's by a relative error of at most 0.022.
Values may be sent and summed in bfloat16 or wider, within the bound.
A program may use at most 320 MiB of HBM per device.

v0:
```python
import jax
import jax.numpy as jnp
from jax import lax
from jax.sharding import PartitionSpec as P

HEAD = 64
LEN = 2048


epsilon = 1e-05
masked_value = -1e30


def normed(values, gain_row, shift_row):
    centre = values - jnp.mean(values, axis=-1, keepdims=True)
    spread = jnp.mean(centre * centre, axis=-1, keepdims=True)
    return centre * lax.rsqrt(spread + epsilon) * gain_row + shift_row


def smooth(values):
    return jax.nn.gelu(values, approximate=False)


def across(former, latter):
    return lax.dot_general(
        former, latter, (((0,), (0,)), ((), ())), preferred_element_type=jnp.float32
    )


def against(former, latter):
    return lax.dot_general(
        former, latter, (((1,), (1,)), ((), ())), preferred_element_type=jnp.float32
    )


def column_slice(matrix, column_start, column_count):
    return lax.dynamic_slice_in_dim(matrix, column_start, column_count, 1)


def head_logits(queries, keys, seen, head_size):
    query_rows = queries.shape[0]
    key_rows = keys.shape[0]
    head_count = queries.shape[1] // head_size
    query_heads = queries.reshape(query_rows, head_count, head_size)
    key_heads = keys.reshape(key_rows, head_count, head_size)
    logits = jnp.einsum(
        "qhd,khd->hqk", query_heads, key_heads, preferred_element_type=jnp.float32
    ) * head_size ** (-0.5)
    return (jnp.where(seen[None], logits, masked_value), query_heads, key_heads)


def attend(queries, keys, values, seen, head_size):
    logits, query_heads, key_heads = head_logits(queries, keys, seen, head_size)
    row_max = jnp.max(logits, axis=-1, keepdims=True)
    powers = jnp.exp(logits - row_max)
    denominator = jnp.sum(powers, axis=-1, keepdims=True)
    probs_low = (powers / denominator).astype(jnp.bfloat16)
    value_heads = values.reshape(key_heads.shape)
    mixed = jnp.einsum("hqk,khd->qhd", probs_low, value_heads, preferred_element_type=jnp.float32)
    return (mixed.reshape(queries.shape), (row_max + jnp.log(denominator))[..., 0])


def score_grads(queries, keys, values, seen, settled, upstream, head_size, inner):
    logits, query_heads, key_heads = head_logits(queries, keys, seen, head_size)
    probs = jnp.exp(logits - settled[..., None])
    value_heads = values.reshape(key_heads.shape)
    upstream_heads = upstream.reshape(query_heads.shape)
    grad_probs = jnp.einsum(
        "qhd,khd->hqk", upstream_heads, value_heads, preferred_element_type=jnp.float32
    )
    inner = jnp.sum(probs * grad_probs, axis=-1)
    grad_logits = (probs * (grad_probs - inner[..., None])).astype(jnp.bfloat16)
    return (probs, grad_logits, query_heads, key_heads, upstream_heads, inner)


def attend_back(queries, keys, values, seen, settled, upstream, head_size):
    probs, grad_logits, query_heads, key_heads, upstream_heads, inner = score_grads(
        queries, keys, values, seen, settled, upstream, head_size, None
    )
    factor = head_size ** (-0.5)
    grad_queries = (
        jnp.einsum("hqk,khd->qhd", grad_logits, key_heads, preferred_element_type=jnp.float32)
        * factor
    )
    grad_keys = (
        jnp.einsum("hqk,qhd->khd", grad_logits, query_heads, preferred_element_type=jnp.float32)
        * factor
    )
    grad_values = jnp.einsum(
        "hqk,qhd->khd",
        probs.astype(jnp.bfloat16),
        upstream_heads,
        preferred_element_type=jnp.float32,
    )
    return (
        grad_queries.reshape(queries.shape),
        grad_keys.reshape(keys.shape),
        grad_values.reshape(keys.shape),
    )


def per_device(
    inputs,
    prefix,
    qkv_weight,
    qv_bias,
    out_weight,
    branch_bias,
    up_weight,
    up_bias,
    down_weight,
    norm_gain,
    norm_bias,
    cotangent,
):
    shard_count = lax.axis_size("shard")
    shard_place = lax.axis_index("shard")
    batch_count = inputs.shape[0]
    token_rows = inputs.shape[2]
    feature_count = inputs.shape[3]
    hidden_count = up_bias.shape[0] * shard_count
    head_size = HEAD
    group_heads = min(4, feature_count // head_size)
    group_width = group_heads * head_size
    group_count = feature_count // group_width
    group_rows = token_rows * shard_count
    first_row = shard_place * token_rows
    seq_index = first_row // LEN
    seq_offset = seq_index * LEN
    query_pos = first_row - seq_offset + jnp.arange(token_rows, dtype=jnp.int32)
    key_pos = jnp.arange(LEN, dtype=jnp.int32)
    group_ids = jnp.arange(group_count, dtype=jnp.int32)
    full_shapes = (
        (feature_count, 3 * feature_count),
        (2, feature_count),
        (feature_count, feature_count),
        (2, feature_count),
        (feature_count, hidden_count),
        (hidden_count,),
        (hidden_count, feature_count),
        (4, feature_count),
        (4, feature_count),
    )
    running = tuple((jnp.zeros(array_shape, jnp.float32) for array_shape in full_shapes))
    outputs = []
    input_grads = []
    for batch_index in range(batch_count):
        qkv_full = lax.all_gather(qkv_weight, "shard", axis=0, tiled=True)
        qvbias_full = lax.all_gather(qv_bias, "shard", axis=1, tiled=True)
        out_full = lax.all_gather(out_weight, "shard", axis=0, tiled=True)
        branch_full = lax.all_gather(branch_bias, "shard", axis=1, tiled=True)
        up_full = lax.all_gather(up_weight, "shard", axis=0, tiled=True)
        upbias_full = lax.all_gather(up_bias, "shard", axis=0, tiled=True)
        down_full = lax.all_gather(down_weight, "shard", axis=0, tiled=True)
        gain_full = lax.all_gather(norm_gain, "shard", axis=1, tiled=True)
        shift_full = lax.all_gather(norm_bias, "shard", axis=1, tiled=True)
        biases_qv = qvbias_full.astype(jnp.float32)
        biases_branch = branch_full.astype(jnp.float32)
        biases_up = upbias_full.astype(jnp.float32)
        gains = gain_full.astype(jnp.float32)
        shifts = shift_full.astype(jnp.float32)
        tokens = inputs[batch_index, 0].astype(jnp.float32)
        prefix_row = prefix[batch_index, 0]
        prefix_len = jnp.sum(
            jnp.where(jnp.arange(prefix_row.shape[0], dtype=jnp.int32) == seq_index, prefix_row, 0)
        )
        seen = (key_pos[None, :] <= query_pos[:, None]) | (key_pos[None, :] < prefix_len)
        normal_in, pull_in = jax.vjp(normed, tokens, gains[0], shifts[0])
        normal_low = normal_in.astype(jnp.bfloat16)
        joined = jnp.dot(normal_low, qkv_full, preferred_element_type=jnp.float32)
        queries = (joined[:, :feature_count] + biases_qv[0]).astype(jnp.bfloat16)
        keys_own = joined[:, feature_count : 2 * feature_count].astype(jnp.bfloat16)
        values_own = (joined[:, 2 * feature_count :] + biases_qv[1]).astype(jnp.bfloat16)
        keys_group = lax.all_gather(keys_own, "shard", axis=0, tiled=True)
        values_group = lax.all_gather(values_own, "shard", axis=0, tiled=True)
        keys = lax.dynamic_slice_in_dim(keys_group, seq_offset, LEN, 0)
        values = lax.dynamic_slice_in_dim(values_group, seq_offset, LEN, 0)

        def forward_group(group_id):
            column_start = group_id * group_width
            return attend(
                column_slice(queries, column_start, group_width),
                column_slice(keys, column_start, group_width),
                column_slice(values, column_start, group_width),
                seen,
                head_size,
            )

        mixed_parts, settled = lax.map(forward_group, group_ids)
        mixed_low = (
            mixed_parts.transpose(1, 0, 2).reshape(token_rows, feature_count).astype(jnp.bfloat16)
        )
        branch = jnp.dot(mixed_low, out_full, preferred_element_type=jnp.float32) + biases_branch[0]
        side, pull_side = jax.vjp(normed, branch, gains[1], shifts[1])
        stream = tokens + side
        normal_mid, pull_mid = jax.vjp(normed, stream, gains[2], shifts[2])
        middle_low = normal_mid.astype(jnp.bfloat16)
        upper = jnp.dot(middle_low, up_full, preferred_element_type=jnp.float32) + biases_up
        active, pull_active = jax.vjp(smooth, upper)
        active_low = active.astype(jnp.bfloat16)
        lower = (
            jnp.dot(active_low, down_full, preferred_element_type=jnp.float32) + biases_branch[1]
        )
        closing, pull_close = jax.vjp(normed, lower, gains[3], shifts[3])
        output = (stream + closing).astype(jnp.bfloat16)
        upstream = cotangent[batch_index, 0].astype(jnp.float32)
        grad_lower, gain_three, shift_three = pull_close(upstream)
        lower_low = grad_lower.astype(jnp.bfloat16)
        grad_active = against(lower_low, down_full)
        (grad_upper,) = pull_active(grad_active)
        upper_low = grad_upper.astype(jnp.bfloat16)
        grad_middle = against(upper_low, up_full)
        grad_mid_in, gain_two, shift_two = pull_mid(grad_middle)
        grad_stream = grad_mid_in + upstream
        grad_branch, gain_one, shift_one = pull_side(grad_stream)
        branch_low = grad_branch.astype(jnp.bfloat16)
        grad_mixed = against(branch_low, out_full).astype(jnp.bfloat16)

        def backward_group(group_item):
            group_id, group_settled = group_item
            column_start = group_id * group_width
            return attend_back(
                column_slice(queries, column_start, group_width),
                column_slice(keys, column_start, group_width),
                column_slice(values, column_start, group_width),
                seen,
                group_settled,
                column_slice(grad_mixed, column_start, group_width),
                head_size,
            )

        query_parts, key_parts, value_parts = lax.map(backward_group, (group_ids, settled))
        grad_queries = (
            query_parts.transpose(1, 0, 2).reshape(token_rows, feature_count).astype(jnp.bfloat16)
        )
        key_terms = key_parts.transpose(1, 0, 2).reshape(LEN, feature_count)
        value_terms = value_parts.transpose(1, 0, 2).reshape(LEN, feature_count)
        empty_rows = jnp.zeros((group_rows, feature_count), jnp.float32)
        key_group_terms = lax.dynamic_update_slice_in_dim(empty_rows, key_terms, seq_offset, 0)
        value_group_terms = lax.dynamic_update_slice_in_dim(empty_rows, value_terms, seq_offset, 0)
        grad_keys = lax.psum_scatter(
            key_group_terms.astype(jnp.bfloat16), "shard", scatter_dimension=0, tiled=True
        )
        grad_values = lax.psum_scatter(
            value_group_terms.astype(jnp.bfloat16), "shard", scatter_dimension=0, tiled=True
        )
        joined_low = jnp.concatenate([grad_queries, grad_keys, grad_values], axis=1)
        grad_normal = against(joined_low, qkv_full)
        grad_tokens, gain_zero, shift_zero = pull_in(grad_normal)
        input_grad = (grad_stream + grad_tokens).astype(jnp.bfloat16)
        gradients = (
            across(normal_low, joined_low),
            jnp.stack(
                [
                    jnp.sum(grad_queries.astype(jnp.float32), axis=0),
                    jnp.sum(grad_values.astype(jnp.float32), axis=0),
                ]
            ),
            across(mixed_low, branch_low),
            jnp.stack(
                [
                    jnp.sum(branch_low.astype(jnp.float32), axis=0),
                    jnp.sum(lower_low.astype(jnp.float32), axis=0),
                ]
            ),
            across(middle_low, upper_low),
            jnp.sum(upper_low.astype(jnp.float32), axis=0),
            across(active_low, lower_low),
            jnp.stack([gain_zero, gain_one, gain_two, gain_three]),
            jnp.stack([shift_zero, shift_one, shift_two, shift_three]),
        )
        output, input_grad, gradients = (output, input_grad, gradients)
        outputs.append(output[None, None])
        input_grads.append(input_grad[None, None])
        running = tuple((former + latter for former, latter in zip(running, gradients)))
    running = (
        lax.psum_scatter(
            running[0].astype(jnp.bfloat16), "shard", scatter_dimension=0, tiled=True
        ).astype(jnp.float32),
        lax.psum_scatter(
            running[1].astype(jnp.bfloat16), "shard", scatter_dimension=1, tiled=True
        ).astype(jnp.float32),
        lax.psum_scatter(
            running[2].astype(jnp.bfloat16), "shard", scatter_dimension=0, tiled=True
        ).astype(jnp.float32),
        lax.psum_scatter(
            running[3].astype(jnp.bfloat16), "shard", scatter_dimension=1, tiled=True
        ).astype(jnp.float32),
        lax.psum_scatter(
            running[4].astype(jnp.bfloat16), "shard", scatter_dimension=0, tiled=True
        ).astype(jnp.float32),
        lax.psum_scatter(
            running[5].astype(jnp.bfloat16), "shard", scatter_dimension=0, tiled=True
        ).astype(jnp.float32),
        lax.psum_scatter(
            running[6].astype(jnp.bfloat16), "shard", scatter_dimension=0, tiled=True
        ).astype(jnp.float32),
        lax.psum_scatter(
            running[7].astype(jnp.bfloat16), "shard", scatter_dimension=1, tiled=True
        ).astype(jnp.float32),
        lax.psum_scatter(
            running[8].astype(jnp.bfloat16), "shard", scatter_dimension=1, tiled=True
        ).astype(jnp.float32),
    )
    summed = (
        lax.psum(running[0].astype(jnp.bfloat16), "replica").astype(jnp.float32),
        lax.psum(running[1].astype(jnp.bfloat16), "replica").astype(jnp.float32),
        lax.psum(running[2].astype(jnp.bfloat16), "replica").astype(jnp.float32),
        lax.psum(running[3].astype(jnp.bfloat16), "replica").astype(jnp.float32),
        lax.psum(running[4].astype(jnp.bfloat16), "replica").astype(jnp.float32),
        lax.psum(running[5].astype(jnp.bfloat16), "replica").astype(jnp.float32),
        lax.psum(running[6].astype(jnp.bfloat16), "replica").astype(jnp.float32),
        lax.psum(running[7].astype(jnp.bfloat16), "replica").astype(jnp.float32),
        lax.psum(running[8].astype(jnp.bfloat16), "replica").astype(jnp.float32),
    )
    return (
        jnp.concatenate(outputs, axis=0),
        jnp.concatenate(input_grads, axis=0),
        summed[0],
        summed[1],
        summed[2],
        summed[3],
        summed[4],
        summed[5],
        summed[6],
        summed[7],
        summed[8],
    )


def solution(mesh):
    placed = (
        P(None, "replica", "shard", None),
        P(None, "replica", None),
        P("shard", None),
        P(None, "shard"),
        P("shard", None),
        P(None, "shard"),
        P("shard", None),
        P("shard"),
        P("shard", None),
        P(None, "shard"),
        P(None, "shard"),
        P(None, "replica", "shard", None),
    )
    return jax.shard_map(
        per_device,
        mesh=mesh,
        in_specs=placed,
        out_specs=(
            P(None, "replica", "shard", None),
            P(None, "replica", "shard", None),
            P("shard", None),
            P(None, "shard"),
            P("shard", None),
            P(None, "shard"),
            P("shard", None),
            P("shard"),
            P("shard", None),
            P(None, "shard"),
            P(None, "shard"),
        ),
        check_vma=False,
    )
```

profile of v0, /device:TPU:0, one launch (start us, length us, event | category | flops | bytes accessed | tf_op | source)
XLA Modules:
  0.0 2096.7 jit_solution(11521051446472900715)
XLA Ops:
  8.0 22.5 %all_gather.51 = bf16[2,1024]{1,0:T(2,128)(2,1)S(1)} all-gather(bf16[2,128]{1,0:T(2,128)(2,1)} %param.23), channel_id=1, replica_groups=mesh['shard'=8,'replica'=4] {'shard'}, dimensions={1}, use_global_device_ids=true | all-gather | bytes 4608 | tf_op jit(solution)/shard_map/all_gather | solution.py:149
  30.5 17.0 all_gather.48
  47.5 18.5 all_gather.49
  70.3 41.8 %all-gather.10.cloned.1.call-done = bf16[1024,3072]{1,0:T(8,128)(2,1)} async-done(((bf16[128,3072]{1,0:T(8,128)(2,1)}), bf16[1024,3072]{1,0:T(8,128)(2,1)}) %all-gather.10.cloned.1.call-update) | async-done | bytes 6291472 | tf_op jit(solution)/shard_map/all_gather | solution.py:148
  129.7 17.9 all_gather.55
  148.9 26.5 %all-gather = bf16[8,1,512]{2,1,0:T(2,128)(2,1)S(1)} all-gather(bf16[1,1,512]{2,1,0:T(2,128)(2,1)S(1)} %reshape.475), channel_id=1, replica_groups=mesh['shard'=8,'replica'=4] {'shard'}, dimensions={0}, use_global_device_ids=true | all-gather | bytes 9216 | tf_op jit(solution)/shard_map/all_gather | solution.py:153
  178.5 16.2 all-gather.22.cloned.1.call-done
  201.4 67.6 %all-gather.24.cloned.1.call-done = bf16[2048,1024]{1,0:T(8,128)(2,1)} async-done(((bf16[256,1024]{1,0:T(8,128)(2,1)}), bf16[2048,1024]{1,0:T(8,128)(2,1)}) %all-gather.24.cloned.1.call-update) | async-done | bytes 4194320 | tf_op jit(solution)/shard_map/all_gather | solution.py:174
  275.6 41.1 %while.57 = (s32[]{:T(128)}, bf16[4,256,256]{1,2,0:T(8,128)(2,1)S(1)}, f32[4,4,256]{2,1,0:T(4,128)S(1)}, s32[4]{0:T(128)S(1)}, bf16[2048,1024]{0,1:T(8,128)(2,1)...) while((s32[]{:T(128)}, ...), condition=%wide.region_17.18_spmd.clone, body=%wide.region_14.17_spmd.clone.sunk | while | flops 563084288 | bytes 34376904 | solution.py:189
  321.3 71.8 %all-gather.12.cloned.1.call-done = bf16[2048,1024]{1,0:T(8,128)(2,1)} async-done(((bf16[256,1024]{1,0:T(8,128)(2,1)}), bf16[2048,1024]{1,0:T(8,128)(2,1)}) %all-gather.12.cloned.1.call-update) | async-done | bytes 4194320 | tf_op jit(solution)/shard_map/all_gather | solution.py:175
  399.6 67.8 %all-gather.14.cloned.1.call-done = bf16[2048,1024]{1,0:T(8,128)(2,1)} async-done(((bf16[256,1024]{1,0:T(8,128)(2,1)}), bf16[2048,1024]{1,0:T(8,128)(2,1)}) %all-gather.14.cloned.1.call-update) | async-done | bytes 4194320 | tf_op jit(solution)/shard_map/all_gather | solution.py:174
  473.9 41.7 %while.56 = (s32[]{:T(128)}, bf16[4,256,256]{1,2,0:T(8,128)(2,1)S(1)}, f32[4,4,256]{2,1,0:T(4,128)S(1)}, s32[4]{0:T(128)S(1)}, bf16[2048,1024]{0,1:T(8,128)(2,1)...) while((s32[]{:T(128)}, ...), condition=%wide.region_5.6_spmd.clone, body=%wide.region_2.5_spmd.clone.sunk | while | flops 563084288 | bytes 34376904 | solution.py:189
  520.8 71.9 %all-gather.18.cloned.1.call-done = bf16[1024,4096]{1,0:T(8,128)(2,1)} async-done(((bf16[128,4096]{1,0:T(8,128)(2,1)}), bf16[1024,4096]{1,0:T(8,128)(2,1)}) %all-gather.18.cloned.1.call-update) | async-done | bytes 8388624 | tf_op jit(solution)/shard_map/all_gather | solution.py:152
  592.7 16.3 multiply_convert_fusion.2
  609.0 108.9 %all-gather.20.cloned.1.call-done = bf16[4096,1024]{1,0:T(8,128)(2,1)} async-done(((bf16[512,1024]{1,0:T(8,128)(2,1)}), bf16[4096,1024]{1,0:T(8,128)(2,1)}) %all-gather.20.cloned.1.call-update) | async-done | bytes 8388624 | tf_op jit(solution)/shard_map/all_gather | solution.py:154
  725.1 16.5 multiply_convert_fusion.3
  749.4 11.8 convert_reduce_fusion
  798.0 99.4 %while.58 = (s32[]{:T(128)}, bf16[4,256,256]{1,2,0:T(8,128)(2,1)S(1)}, bf16[4,2048,256]{1,2,0:T(8,128)(2,1)}, bf16[4,2048,256]{1,2,0:T(8,128)(2,1)}, s32[4]{0:T(...) while((s32[]{:T(128)}, ...), condition=%wide.region_32.33_spmd.clone, body=%wide.region_30.32_spmd.clone.sunk | while | flops 1375861760 | bytes 105545496 | solution.py:232
  906.3 102.0 %while.59 = (s32[]{:T(128)}, bf16[4,256,256]{1,2,0:T(8,128)(2,1)S(1)}, bf16[4,2048,256]{1,2,0:T(8,128)(2,1)}, bf16[4,2048,256]{1,2,0:T(8,128)(2,1)}, s32[4]{0:T(...) while((s32[]{:T(128)}, ...), condition=%wide.region_45.46_spmd.clone, body=%wide.region_43.45_spmd.clone.sunk | while | flops 1375861760 | bytes 105545496 | solution.py:232
  1057.6 19.6 reduce-scatter.23.cloned.1.call-done
  1085.0 84.0 %reduce-scatter.25.cloned.1.call-done = bf16[256,1024]{0,1:T(8,128)(2,1)} async-done(((bf16[2048,1024]{0,1:T(8,128)(2,1)}), bf16[256,1024]{0,1:T(8,128)(2,1)}) %reduce-scatter.25.cloned.1.call-update) | async-done | bytes 524304 | tf_op jit(solution)/shard_map/reduce_scatter | solution.py:241
  1169.0 92.2 %reduce-scatter.27.cloned.1.call-done = bf16[256,1024]{0,1:T(8,128)(2,1)} async-done(((bf16[2048,1024]{0,1:T(8,128)(2,1)}), bf16[256,1024]{0,1:T(8,128)(2,1)}) %reduce-scatter.27.cloned.1.call-update) | async-done | bytes 524304 | tf_op jit(solution)/shard_map/reduce_scatter | solution.py:244
  1291.6 41.4 %reduce-scatter.31.cloned.1.call-done = bf16[128,1024]{1,0:T(8,128)(2,1)} async-done(((bf16[1024,1024]{1,0:T(8,128)(2,1)}), bf16[128,1024]{1,0:T(8,128)(2,1)}) %reduce-scatter.31.cloned.1.call-update) | async-done | bytes 262160 | tf_op jit(solution)/shard_map/reduce_scatter | solution.py:283
  1333.0 151.5 %reduce-scatter.35.cloned.1.call-done = bf16[512,1024]{1,0:T(8,128)(2,1)} async-done(((bf16[4096,1024]{1,0:T(8,128)(2,1)}), bf16[512,1024]{1,0:T(8,128)(2,1)}) %reduce-scatter.35.cloned.1.call-update) | async-done | bytes 1048592 | tf_op jit(solution)/shard_map/reduce_scatter | solution.py:295
  1484.5 152.0 %reduce-scatter.33.cloned.1.call-done = bf16[128,4096]{1,0:T(8,128)(2,1)} async-done(((bf16[1024,4096]{1,0:T(8,128)(2,1)}), bf16[128,4096]{1,0:T(8,128)(2,1)}) %reduce-scatter.33.cloned.1.call-update) | async-done | bytes 1048592 | tf_op jit(solution)/shard_map/reduce_scatter | solution.py:289
  1636.5 120.4 %reduce-scatter.29.cloned.1.call-done = bf16[128,3072]{1,0:T(8,128)(2,1)} async-done(((bf16[1024,3072]{1,0:T(8,128)(2,1)}), bf16[128,3072]{1,0:T(8,128)(2,1)}) %reduce-scatter.29.cloned.1.call-update) | async-done | bytes 786448 | tf_op jit(solution)/shard_map/reduce_scatter | solution.py:277
  1758.2 19.9 all-reduce
  1780.5 40.0 %reduce-scatter.39.cloned.1.call-done = bf16[128,2]{1,0:T(8,128)(2,1)} async-done(((bf16[1024,2]{1,0:T(8,128)(2,1)}), bf16[128,2]{1,0:T(8,128)(2,1)}) %reduce-scatter.39.cloned.1.call-update) | async-done | bytes 528
  1824.7 59.2 %reduce-scatter.37.cloned.1.call-done = bf16[128,2]{1,0:T(8,128)(2,1)} async-done(((bf16[1024,2]{1,0:T(8,128)(2,1)}), bf16[128,2]{1,0:T(8,128)(2,1)}) %reduce-scatter.37.cloned.1.call-update) | async-done | bytes 528
  1884.8 62.8 %reduce-scatter.43.cloned.1.call-done = bf16[128,4]{1,0:T(8,128)(2,1)} async-done(((bf16[1024,4]{1,0:T(8,128)(2,1)}), bf16[128,4]{1,0:T(8,128)(2,1)}) %reduce-scatter.43.cloned.1.call-update) | async-done | bytes 1040
  1948.4 62.7 %reduce-scatter.41.cloned.1.call-done = bf16[128,4]{1,0:T(8,128)(2,1)} async-done(((bf16[1024,4]{1,0:T(8,128)(2,1)}), bf16[128,4]{1,0:T(8,128)(2,1)}) %reduce-scatter.41.cloned.1.call-update) | async-done | bytes 1040
  2020.4 61.3 %all-reduce.5.cloned.1.call-done = (bf16[128,3072]{1,0:T(8,128)(2,1)}, bf16[128,1024]{1,0:T(8,128)(2,1)}, bf16[128,4096]{1,0:T(8,128)(2,1)}, bf16[512,1024]{1,0:T(8,128)(2,1)}) async-done(((bf16[128,3072]{1,0:T(8,128)(2,1)}, bf16[128,1024]{1,0:T(8,128)(2,1)}, bf16[128,4096]{1,0:T(8,128)(2,1)}, bf16[512,1024]{1,0:T(8,128)(2,1)}), (bf16[128,3072]{1,0:T(8,128)(2,1)}, bf16[128,1024]{1,0:T(8,128)(2,1)}, ...) | async-done | bytes 3145744 | tf_op jit(solution)/shard_map/psum | solution.py:306
  (638 shorter events, 505.6 us)
Async XLA Ops:
  7.2 104.9 %all-gather.10.cloned.1.call-start = ((), (), s32[]{:S(2)}) async-start(), calls=%async_computation.12 | async-start | bytes 7077888 | tf_op jit(solution)/shard_map/all_gather | solution.py:148
  7.9 186.8 %all-gather.22.cloned.1.call-start = ((), (), s32[]{:S(2)}) async-start(), calls=%async_computation.18 | async-start | bytes 4718592 | tf_op jit(solution)/shard_map/all_gather | solution.py:175
  122.6 146.4 %all-gather.24.cloned.1.call-start = ((), (), s32[]{:S(2)}) async-start(), calls=%async_computation.19 | async-start | bytes 4718592 | tf_op jit(solution)/shard_map/all_gather | solution.py:174
  124.8 193.8 %all-gather.16.cloned.1.call-start = ((), (), s32[]{:S(2)}) async-start(), calls=%async_computation.15 | async-start | bytes 2359296 | tf_op jit(solution)/shard_map/all_gather | solution.py:150
  125.4 267.7 %all-gather.12.cloned.1.call-start = ((), (), s32[]{:S(2)}) async-start(), calls=%async_computation.13 | async-start | bytes 4718592 | tf_op jit(solution)/shard_map/all_gather | solution.py:175
  125.9 341.4 %all-gather.14.cloned.1.call-start = ((), (), s32[]{:S(2)}) async-start(), calls=%async_computation.14 | async-start | bytes 4718592 | tf_op jit(solution)/shard_map/all_gather | solution.py:174
  126.9 465.8 %all-gather.18.cloned.1.call-start = ((), (), s32[]{:S(2)}) async-start(), calls=%async_computation.16 | async-start | bytes 9437184 | tf_op jit(solution)/shard_map/all_gather | solution.py:152
  127.6 590.3 %all-gather.20.cloned.1.call-start = ((), (), s32[]{:S(2)}) async-start(), calls=%async_computation.17 | async-start | bytes 9437184 | tf_op jit(solution)/shard_map/all_gather | solution.py:154
  128.4 929.2 %reduce-scatter.21.cloned.1.call-start = ((), (), s32[]{:S(2)}) async-start(), calls=%async_computation.20 | async-start | bytes 4718592 | tf_op jit(solution)/shard_map/reduce_scatter | solution.py:241
  519.5 267.6 %copy-start.3 = (f32[256,1024]{1,0:T(8,128)}, f32[256,1024]{1,0:T(8,128)S(1)}, u32[]{:S(2)}) copy-start(f32[256,1024]{1,0:T(8,128)S(1)} %get-tuple-element.565) | copy-start | bytes 3145732
  519.6 267.6 %copy-start.84 = (f32[256]{0:T(256)}, f32[256]{0:T(256)S(1)}, u32[]{:S(2)}) copy-start(f32[256]{0:T(256)S(1)} %broadcast_multiply_fusion.1) | copy-start | bytes 3076
  520.8 266.4 %copy-start.90 = (f32[256]{0:T(256)}, f32[256]{0:T(256)S(1)}, u32[]{:S(2)}) copy-start(f32[256]{0:T(256)S(1)} %fusion.107) | copy-start | bytes 3076
  592.7 125.3 %copy-start.96 = (f32[1,1024]{1,0:T(1,128)S(1)}, f32[1,1024]{1,0:T(1,128)}, u32[]{:S(2)}) copy-start(f32[1,1024]{1,0:T(1,128)} %get-tuple-element.620) | copy-start | bytes 12292
  898.3 178.8 %reduce-scatter.23.cloned.1.call-start = ((), (), s32[]{:S(2)}) async-start(), calls=%async_computation.21 | async-start | bytes 4718592 | tf_op jit(solution)/shard_map/reduce_scatter | solution.py:244
  898.9 270.1 %reduce-scatter.25.cloned.1.call-start = ((), (), s32[]{:S(2)}) async-start(), calls=%async_computation.22 | async-start | bytes 4718592 | tf_op jit(solution)/shard_map/reduce_scatter | solution.py:241
  1008.3 252.9 %reduce-scatter.27.cloned.1.call-start = ((), (), s32[]{:S(2)}) async-start(), calls=%async_computation.23 | async-start | bytes 4718592 | tf_op jit(solution)/shard_map/reduce_scatter | solution.py:244
  1008.9 324.1 %reduce-scatter.31.cloned.1.call-start = ((), (), s32[]{:S(2)}) async-start(), calls=%async_computation.25 | async-start | bytes 2359296 | tf_op jit(solution)/shard_map/reduce_scatter | solution.py:283
  1012.4 472.2 %reduce-scatter.35.cloned.1.call-start = ((), (), s32[]{:S(2)}) async-start(), calls=%async_computation.27 | async-start | bytes 9437184 | tf_op jit(solution)/shard_map/reduce_scatter | solution.py:295
  1034.3 602.2 %reduce-scatter.33.cloned.1.call-start = ((), (), s32[]{:S(2)}) async-start(), calls=%async_computation.26 | async-start | bytes 9437184 | tf_op jit(solution)/shard_map/reduce_scatter | solution.py:289
  1057.2 699.7 %reduce-scatter.29.cloned.1.call-start = ((), (), s32[]{:S(2)}) async-start(), calls=%async_computation.24 | async-start | bytes 7077888 | tf_op jit(solution)/shard_map/reduce_scatter | solution.py:277
  1077.2 184.0 %copy-start.60 = (f32[256]{0:T(256)S(1)}, f32[256]{0:T(256)}, u32[]{:S(2)}) copy-start(f32[256]{0:T(256)} %copy-done.59) | copy-start | bytes 3076
  1077.2 184.0 %copy-start.66 = (f32[256]{0:T(256)S(1)}, f32[256]{0:T(256)}, u32[]{:S(2)}) copy-start(f32[256]{0:T(256)} %copy-done.65) | copy-start | bytes 3076
  1270.8 549.7 %reduce-scatter.39.cloned.1.call-start = ((), (), s32[]{:S(2)}) async-start(), calls=%async_computation.29 | async-start | bytes 294912
  1273.6 610.3 %reduce-scatter.37.cloned.1.call-start = ((), (), s32[]{:S(2)}) async-start(), calls=%async_computation.28 | async-start | bytes 294912
  1285.8 471.2 %copy-start.102 = (u32[32]{0:T(128)S(1)}, u32[32]{0:T(128)}, u32[]{:S(2)}) copy-start(u32[32]{0:T(128)} %constant.232) | copy-start | bytes 388
  1285.8 472.4 %copy-start.80 = (f32[4096]{0:T(1024)S(1)}, f32[4096]{0:T(1024)}, u32[]{:S(2)}) copy-start(f32[4096]{0:T(1024)} %get-tuple-element.536) | copy-start | bytes 49156
  1285.8 472.4 %copy-start.81 = (f32[4096]{0:T(1024)S(1)}, f32[4096]{0:T(1024)}, u32[]{:S(2)}) copy-start(f32[4096]{0:T(1024)} %get-tuple-element.538) | copy-start | bytes 49156
  1286.7 660.8 %reduce-scatter.43.cloned.1.call-start = ((), (), s32[]{:S(2)}) async-start(), calls=%async_computation.31 | async-start | bytes 294912
  1287.8 723.2 %reduce-scatter.41.cloned.1.call-start = ((), (), s32[]{:S(2)}) async-start(), calls=%async_computation.30 | async-start | bytes 294912
  1287.8 533.5 %copy-start.11 = (f32[256,1024]{1,0:T(8,128)S(1)}, f32[256,1024]{1,0:T(8,128)}, u32[]{:S(2)}) copy-start(f32[256,1024]{1,0:T(8,128)} %copy-done.10) | copy-start | bytes 3145732
  1287.9 533.5 %copy-start.13 = (f32[256,1024]{1,0:T(8,128)S(1)}, f32[256,1024]{1,0:T(8,128)}, u32[]{:S(2)}) copy-start(f32[256,1024]{1,0:T(8,128)} %copy-done.12) | copy-start | bytes 3145732
  1291.5 790.1 %all-reduce.5.cloned.1.call-start = ((), (), s32[]{:S(2)}) async-start(), calls=%async_computation.32 | async-start | bytes 6291456 | tf_op jit(solution)/shard_map/psum | solution.py:306
  (112 other events, 1579.6 us)
Sparse Core Ops, SparseCore 0:
  10.2 101.8 all-gather.9
  122.7 71.9 all-gather.21
  197.4 71.5 all-gather.23
  271.0 47.5 all-gather.15
  321.2 71.8 all-gather.11
  395.6 71.6 all-gather.13
  469.5 123.1 all-gather.17
  594.8 123.1 all-gather.19
  898.5 86.4 reduce-scatter.20
  988.9 88.2 reduce-scatter.22
  1080.8 88.2 reduce-scatter.24
  1172.9 88.2 reduce-scatter.26
  1265.3 67.6 reduce-scatter.30
  1336.5 147.9 reduce-scatter.34
  1488.4 147.9 reduce-scatter.32
  1639.9 116.9 reduce-scatter.28
  1760.1 60.3 reduce-scatter.38
  1823.7 60.2 reduce-scatter.36
  1887.3 60.2 reduce-scatter.42
  1950.7 60.2 reduce-scatter.40
  2013.6 67.9 all-reduce.4
where the time goes:
time: 2100 us
  waiting for transfers between devices  1400 us (67%)
  matrix products  328 us (16%)
  blocking collectives  128 us (6%)
  local copies, waits for them, and re-layouts  127 us (6%)
  other arithmetic  82.3 us (4%)
    unnamed x25, waiting for transfers between devices  229 us
    reduce_scatter x1, waiting for transfers between devices, per_device(): lax.psum_scatter(running[4].astype(jnp.bfloat16), 'shard', scatter_dimens...  152 us
    reduce_scatter x1, waiting for transfers between devices, per_device(): lax.psum_scatter(running[6].astype(jnp.bfloat16), 'shard', scatter_dimens...  151 us
    all_gather x2, waiting for transfers between devices, per_device(): keys_group = lax.all_gather(keys_own, 'shard', axis=0, tiled=True)  135 us
    reduce_scatter x1, waiting for transfers between devices, per_device(): lax.psum_scatter(running[0].astype(jnp.bfloat16), 'shard', scatter_dimens...  120 us
    reduce_scatter x2, waiting for transfers between devices, per_device(): lax.psum_scatter(value_group_terms.astype(jnp.bfloat16), 'shard', scatter...  112 us
    all_gather x1, waiting for transfers between devices, per_device(): down_full = lax.all_gather(down_weight, 'shard', axis=0, tiled=True)  109 us
    all_gather x2, waiting for transfers between devices, per_device(): values_group = lax.all_gather(values_own, 'shard', axis=0, tiled=True)  88 us
  transfers between devices with their start and end apart: 21, of which 20 were waited for; matrix products, arithmetic and copies ran while one was open for 16% of the time, Pallas kernels for 0%

commit v1 on v0

v1 whole, which is shorter than its diff:
```python
import functools
import math

import jax
import jax.numpy as jnp
from jax import lax
from jax.experimental import pallas as pl
from jax.experimental.pallas import tpu as pltpu
from jax.sharding import PartitionSpec as P

HEAD = 64
LEN = 2048
CORES = 2
PAIR = 2 * HEAD
BQ = 256
EPS = 1e-05
MASKED = -1e30
SCALE = HEAD ** (-0.5)
SCALE2 = SCALE * math.log2(math.e)
F32 = jnp.float32
BF16 = jnp.bfloat16
MESH = pl.DeviceIdType.MESH
VMEM_LIMIT = 66_000_000


class Plan:
    def __init__(self, mesh_shape, inputs_shape):
        self.S = mesh_shape["shard"]
        self.R = mesh_shape["replica"]
        self.M, _, self.T, self.D = inputs_shape
        self.Q = self.T * self.S // LEN
        self.P = LEN // self.T
        self.U = self.M * self.Q * CORES
        self.cpu = self.S // self.U
        self.heads = self.D // HEAD
        self.W = self.D // (CORES * self.cpu)
        self.pairs = self.W // PAIR
        self.groups = CORES * self.cpu
        self.pieces = self.T // BQ
        self.nq = LEN // BQ


class Place:
    def __init__(self, plan):
        self.p = plan
        self.s = lax.axis_index("shard")
        self.r = lax.axis_index("replica")
        self.c = lax.rem(self.r, CORES)
        self.chip = self.r - self.c
        self.mate = self.chip + (1 - self.c)
        self.unit = self.s // plan.cpu
        self.lane = lax.rem(self.s, plan.cpu)
        self.group = self.c * plan.cpu + self.lane
        self.uc = lax.rem(self.unit, CORES)
        self.um = lax.rem(self.unit // CORES, plan.M)
        self.uq = self.unit // (CORES * plan.M)
        self.ring = self.to_ring(self.s)

    def unit_of(self, c, m, s):
        return ((s // self.p.P) * self.p.M + m) * CORES + c

    def to_ring(self, s):
        half = self.p.S // 2
        row, col = s // 2, lax.rem(s, 2)
        return row + col * (2 * half - 1 - 2 * row)

    def from_ring(self, i):
        n = self.p.S
        return jnp.where(i < n // 2, 2 * i, 2 * (n - 1 - i) + 1)


def remote(src, dst, send, recv, s, r):
    return pltpu.make_async_remote_copy(
        src_ref=src, dst_ref=dst, send_sem=send, recv_sem=recv, device_id=(s, r), device_id_type=MESH
    )


def launch(away, far, near):
    @pl.when(away)
    def _():
        far().start()

    @pl.when(jnp.logical_not(away))
    def _():
        pltpu.make_async_copy(*near).start()


def sent(away, far, near):
    @pl.when(away)
    def _():
        far().wait_send()


def greet(peers):
    barrier = pltpu.get_barrier_semaphore()
    for s, r in peers:
        pl.semaphore_signal(barrier, inc=1, device_id=(s, r), device_id_type=MESH)
    pl.semaphore_wait(barrier, len(peers))


def plane_peers(here):
    n = here.p.S * CORES
    own = here.s * CORES + here.c
    out = []
    for k in range(1, n):
        i = lax.rem(own + k, n)
        out.append((i // CORES, here.chip + lax.rem(i, CORES)))
    return out


def normed(values, gain, shift):
    centre = values - jnp.mean(values, axis=-1, keepdims=True)
    spread = jnp.mean(centre * centre, axis=-1, keepdims=True)
    return centre * lax.rsqrt(spread + EPS) * gain + shift


def dot(a, b, ca=1, cb=0):
    return lax.dot_general(a, b, (((ca,), (cb,)), ((), ())), preferred_element_type=F32)


def head_lanes(rows, which):
    lane = lax.broadcasted_iota(jnp.int32, (rows, PAIR), 1)
    return (lane < HEAD) if which == 0 else (lane >= HEAD)


def fore_kernel(
    plan, x, par, pre, wq, wo, wu, wd,
    wqf, wof, wuf, wdf, parf, ah, q_out, k_out, v_out, o_out, lse_out, preu, oh,
    parg, a_all, wcol, pre2,
    par_ss, par_rs, pre_sem, loc_sem, a_ss, a_rs, af_ss, w_ss, w_rs, wf_ss, wf_rs, o_ss, o_rs, col_sem,
):
    p = plan
    here = Place(p)
    s, c = here.s, here.c
    mine, full = (wq, wo, wu, wd), (wqf, wof, wuf, wdf)
    nw = len(mine)
    steps = p.S - 1
    greet(plane_peers(here))

    parg[s] = par[...]
    small = []
    for k in range(1, p.S):
        to = lax.rem(s + k, p.S)
        small.append(remote(par, parg.at[s], par_ss.at[k], par_rs.at[k], to, here.r))
        small[-1].start()
    swap = remote(pre, pre2, pre_sem.at[0], pre_sem.at[1], s, here.mate)
    swap.start()

    def block(w, origin, core, d):
        n = mine[w].shape[0]
        return pl.ds(pl.multiple_of(origin * n + core * (n // 2) + d * (n // 4), n // 4), n // 4)

    def own_block(w, d):
        n = mine[w].shape[0]
        return pl.ds(pl.multiple_of(c * (n // 2) + d * (n // 4), n // 4), n // 4)

    def origin_of(d, t):
        i = lax.rem(here.ring + (p.S - 1 - t if d == 0 else 1 + t), p.S)
        return here.from_ring(i)

    ahead = [here.from_ring(lax.rem(here.ring + (1 if d == 0 else p.S - 1), p.S)) for d in (0, 1)]

    def ring_first(w):
        for d in (0, 1):
            remote(
                mine[w].at[own_block(w, d), :], full[w].at[block(w, s, c, d), :],
                w_ss.at[w, d, 0], w_rs.at[w, d, 0], ahead[d], here.r,
            ).start()

    def ring_pass(w, d, t):
        rows = block(w, origin_of(d, t), c, d)
        part = full[w].at[rows, :]
        remote(part, part, w_ss.at[w, d, t], w_rs.at[w, d, t], ahead[d], here.r).wait_recv()

        @pl.when(t < steps - 1)
        def _():
            later = jnp.minimum(t + 1, steps - 1)
            remote(part, part, w_ss.at[w, d, later], w_rs.at[w, d, later], ahead[d], here.r).start()

        remote(part, part, wf_ss.at[w, d, t], wf_rs.at[w, d, t], s, here.mate).start()

    def ring_mate(w, d, t):
        part = full[w].at[block(w, origin_of(d, t), 1 - c, d), :]
        return remote(part, part, wf_ss.at[w, d, t], wf_rs.at[w, d, t], s, here.mate)

    ring_first(0)
    local = []
    for w in range(nw):
        n = mine[w].shape[0]
        local.append(
            pltpu.make_async_copy(mine[w], full[w].at[pl.ds(pl.multiple_of(s * n, n), n), :], loc_sem.at[w])
        )
        local[-1].start()

    for k in range(1, p.S):
        small[k - 1].wait_recv()
    parf[...] = jnp.concatenate([parg[k][:, : p.D // p.S] for k in range(p.S)], axis=1)
    gain = parf[4:5, :].astype(F32)
    shift = parf[8:9, :].astype(F32)
    rows_here = pl.ds(pl.multiple_of(lax.rem(s, p.P) * p.T, p.T), p.T)

    def first_hop(m):
        to = here.unit_of(c, m, s) * p.cpu + here.lane
        far = lambda: remote(ah.at[m], a_all.at[rows_here, :], a_ss.at[m], a_rs.at[lax.rem(s, p.P)], to, here.r)
        return to, far

    for m in range(p.M):
        ah[m] = normed(x[m].astype(F32), gain, shift).astype(BF16)
        to, far = first_hop(m)

        @pl.when(to != s)
        def _():
            far().start()

        @pl.when(to == s)
        def _():
            a_all[rows_here, :] = ah[m]

    primary = c == here.uc

    def a_rows(j):
        return pl.ds(pl.multiple_of(j * p.T, p.T), p.T)

    def a_forward(j, k):
        part = a_all.at[a_rows(j), :]
        if k == 0:
            return remote(part, part, af_ss.at[j, 0], a_rs.at[j], s, here.mate)
        to = here.unit * p.cpu + lax.rem(here.lane + k, p.cpu)
        return remote(part, part, af_ss.at[j, k], a_rs.at[j], to, here.r)

    def a_wait(j):
        part = a_all.at[a_rows(j), :]
        remote(part, part, af_ss.at[j, 0], a_rs.at[j], s, here.mate).wait_recv()

    near = p.P // p.cpu

    def a_near(jj):
        @pl.when(primary)
        def _():
            j = jj * p.cpu + here.lane

            @pl.when(here.uq * p.P + j != s)
            def _():
                a_wait(j)

            for k in list(range(1, p.cpu)) + [0]:
                a_forward(j, k).start()

    def a_far(jj):
        @pl.when(primary)
        def _():
            for k in range(1, p.cpu):
                j = jj * p.cpu + lax.rem(here.lane + k, p.cpu)
                a_wait(j)
                a_forward(j, 0).start()

    for t in range(steps):
        for d in (0, 1):
            ring_pass(0, d, t)
        if t < near:
            a_near(t)
        if 2 <= t < near + 2:
            a_far(t - 2)
    for w in range(1, nw):
        ring_first(w)

    @pl.when(jnp.logical_not(primary))
    def _():
        for j in range(p.P):
            a_wait(j)

    swap.wait_recv()
    pre2[...] = jnp.where(primary, pre[...], pre2[...])
    row = here.um * p.Q + here.uq
    preu[...] = jnp.broadcast_to(pre2[pl.ds(row, 1), :], preu.shape)

    for t in range(steps):
        for d in (0, 1):
            ring_mate(0, d, t).wait_recv()
    local[0].wait()
    cols = []
    for k in range(3):
        start = pl.multiple_of(k * p.D + here.group * p.W, PAIR)
        cols.append(pltpu.make_async_copy(wqf.at[:, pl.ds(start, p.W)], wcol.at[k], col_sem.at[k]))
        cols[-1].start()
    for copy in cols:
        copy.wait()
    own = pl.ds(pl.multiple_of(here.group * p.W, PAIR), p.W)
    q_bias = parf[0:1, own].astype(F32)
    v_bias = parf[1:2, own].astype(F32)

    def project(i, carry):
        rows = pl.ds(pl.multiple_of(i * BQ, BQ), BQ)
        part = a_all[rows, :]
        q_out[rows, :] = (dot(part, wcol[0]) + q_bias).astype(BF16)
        k_out[rows, :] = dot(part, wcol[1]).astype(BF16)
        v_out[rows, :] = (dot(part, wcol[2]) + v_bias).astype(BF16)
        return carry

    lax.fori_loop(0, p.nq, project, 0)

    prefix = preu[0:1, 0:1]
    per = -(-steps // p.nq)

    def o_copy(i):
        rows = pl.ds(pl.multiple_of(i * BQ, BQ), BQ)
        home = here.uq * p.P + i // p.pieces
        piece = lax.rem(i, p.pieces)
        there = pl.ds(pl.multiple_of(piece * BQ, BQ), BQ)
        src = o_out.at[rows, :]
        dst = oh.at[here.um, there, own]
        away = jnp.logical_or(home != s, here.uc != c)
        recv = o_rs.at[here.um, here.group, piece]
        return away, lambda: remote(src, dst, o_ss.at[i], recv, home, here.chip + here.uc), (src, dst, recv)

    def attend(i, carry):
        rows = pl.ds(pl.multiple_of(i * BQ, BQ), BQ)
        row_pos = (lax.broadcasted_iota(jnp.int32, (BQ, 1), 0) + i * BQ + 1).astype(F32)
        bound = jnp.maximum(row_pos, prefix)
        key_pos = lax.broadcasted_iota(jnp.int32, (1, LEN), 1).astype(F32)
        seen = key_pos < bound

        def pair_step(h, inner):
            lanes = pl.ds(pl.multiple_of(h * PAIR, PAIR), PAIR)
            qp, kp, vp = q_out[rows, lanes], k_out[:, lanes], v_out[:, lanes]
            halves = []
            for e in (0, 1):
                logits = dot(jnp.where(head_lanes(BQ, e), qp, jnp.zeros_like(qp)), kp, 1, 1)
                logits = jnp.where(seen, logits, MASKED)
                top = jnp.max(logits, axis=1, keepdims=True)
                powers = jnp.exp2((logits - top) * SCALE2)
                total = jnp.sum(powers, axis=1, keepdims=True)
                halves.append(dot(powers.astype(BF16), vp) * (1.0 / total))
                level = top * SCALE2 + jnp.log2(total)
                turned = jnp.broadcast_to(level, (BQ, 128)).T
                lse_out[2 * h + e, :, pl.ds(pl.multiple_of(i * BQ, BQ), BQ)] = turned[0:8]
            o_out[rows, lanes] = jnp.where(head_lanes(BQ, 0), halves[0], halves[1]).astype(BF16)
            return inner

        lax.fori_loop(0, p.pairs, pair_step, 0)
        launch(*o_copy(i))

        for extra in range(per):
            t = i * per + extra

            @pl.when(t < steps)
            def _():
                for w in range(1, nw):
                    for d in (0, 1):
                        ring_pass(w, d, jnp.minimum(t, steps - 1))

        return carry

    lax.fori_loop(0, p.nq, attend, 0)

    for m in range(p.M):
        for g in range(p.groups):
            for piece in range(p.pieces):
                src = o_out.at[pl.ds(0, BQ), :]
                dst = oh.at[m, pl.ds(piece * BQ, BQ), pl.ds(g * p.W, p.W)]
                pltpu.make_async_copy(src, dst, o_rs.at[m, g, piece]).wait()

    def o_sent(i, carry):
        sent(*o_copy(i))
        return carry

    lax.fori_loop(0, p.nq, o_sent, 0)
    for copy in small:
        copy.wait_send()
    swap.wait_send()
    for copy in local[1:]:
        copy.wait()
    for m in range(p.M):
        to, far = first_hop(m)

        @pl.when(to != s)
        def _():
            far().wait_send()

    @pl.when(primary)
    def _():
        for jj in range(near):
            for k in range(p.cpu):
                a_forward(jj * p.cpu + here.lane, k).wait_send()
            for k in range(1, p.cpu):
                a_forward(jj * p.cpu + lax.rem(here.lane + k, p.cpu), 0).wait_send()

    def drain(t, carry):
        for w in range(nw):
            for d in (0, 1):
                if w:
                    ring_mate(w, d, t).wait_recv()
                ring_mate(w, d, t).wait_send()
                part = full[w].at[block(w, origin_of(d, t), c, d), :]
                remote(part, part, w_ss.at[w, d, t], w_rs.at[w, d, t], ahead[d], here.r).wait_send()
        return carry

    lax.fori_loop(0, steps, drain, 0)


def fore(plan, x, par, pre, weights):
    p = plan
    steps = p.S - 1
    nw = len(weights)
    any_space = pl.BlockSpec(memory_space=pl.ANY)
    vmem = pl.BlockSpec(memory_space=pltpu.VMEM)
    shape = jax.ShapeDtypeStruct
    out_shape = (
        [shape((w.shape[0] * p.S, w.shape[1]), BF16) for w in weights]
        + [shape((par.shape[0], p.D), BF16), shape((p.M, p.T, p.D), BF16)]
        + [shape((LEN, p.W), BF16)] * 4
        + [shape((2 * p.pairs, 8, LEN), F32), shape((8, 128), F32), shape((p.M, p.T, p.D), BF16)]
    )
    dma = pltpu.SemaphoreType.DMA
    return pl.pallas_call(
        functools.partial(fore_kernel, p),
        out_shape=out_shape,
        in_specs=[vmem] * (3 + nw),
        out_specs=[any_space] * nw + [vmem] * 9,
        scratch_shapes=[
            pltpu.VMEM((p.S,) + par.shape, BF16),
            pltpu.VMEM((LEN, p.D), BF16),
            pltpu.VMEM((3, p.D, p.W), BF16),
            pltpu.VMEM((8, 128), F32),
            dma((p.S,)), dma((p.S,)), dma((2,)), dma((nw,)),
            dma((p.M,)), dma((p.P,)), dma((p.P, p.cpu)),
            dma((nw, 2, steps)), dma((nw, 2, steps)), dma((nw, 2, steps)), dma((nw, 2, steps)),
            dma((p.nq,)), dma((p.M, p.groups, p.pieces)), dma((3,)),
        ],
        compiler_params=pltpu.CompilerParams(
            collective_id=0, has_side_effects=True, vmem_limit_bytes=VMEM_LIMIT
        ),
        name="fore",
    )(x, par, pre, *weights)


def back_kernel(
    plan, q, k, v, o, lse, preu, dh_home,
    home_out,
    do_all, dq_buf, dkv_buf, dk_acc, dv_acc, k_turn,
    do_ss, do_rs, g_ss, g_rs,
):
    p = plan
    here = Place(p)
    s, c = here.s, here.c
    greet(plane_peers(here))
    rows_here = pl.ds(pl.multiple_of(lax.rem(s, p.P) * p.T, p.T), p.T)

    def do_copy(m, g):
        core, lane = g // p.cpu, g % p.cpu
        to = here.unit_of(c, m, s) * p.cpu + lane
        src = dh_home.at[m, :, pl.ds(g * p.W, p.W)]
        dst = do_all.at[rows_here, :]
        away = jnp.logical_or(to != s, c != core)
        recv = do_rs.at[lax.rem(s, p.P)]
        return away, lambda: remote(src, dst, do_ss.at[m, g], recv, to, here.chip + core), (src, dst, recv)

    for m in range(p.M):
        for g in range(p.groups):
            launch(*do_copy(m, g))

    prefix = preu[0:1, 0:1]
    unit_dev = here.chip + here.uc

    def g_copy(part, h, i):
        rows = pl.ds(pl.multiple_of(i * BQ, BQ), BQ)
        src = dq_buf.at[h, rows, :] if part == 0 else dkv_buf.at[part - 1, h, rows, :]
        home = here.uq * p.P + i // p.pieces
        piece = lax.rem(i, p.pieces)
        there = pl.ds(pl.multiple_of(piece * BQ, BQ), BQ)
        lanes = pl.ds(pl.multiple_of(part * p.D + here.group * p.W + h * PAIR, PAIR), PAIR)
        dst = home_out.at[here.um, there, lanes]
        recv = g_rs.at[part, here.um, here.group * p.pairs + h, piece]
        away = jnp.logical_or(home != s, here.uc != c)
        return away, lambda: remote(src, dst, g_ss.at[part, h, i], recv, home, unit_dev), (src, dst, recv)

    def pair_step(h, carry):
        lanes = pl.ds(pl.multiple_of(h * PAIR, PAIR), PAIR)
        k_turn[...] = k[:, lanes].astype(F32).T.astype(BF16)
        dk_acc[...] = jnp.zeros_like(dk_acc)
        dv_acc[...] = jnp.zeros_like(dv_acc)

        def query_step(i, inner):
            rows = pl.ds(pl.multiple_of(i * BQ, BQ), BQ)

            @pl.when(jnp.logical_and(h == 0, lax.rem(i, p.pieces) == 0))
            def _():
                j = i // p.pieces
                part = do_all.at[pl.ds(pl.multiple_of(j * p.T, p.T), p.T), :]
                pltpu.make_async_copy(part, part, do_rs.at[j]).wait()

            qp, dop, op = q[rows, lanes], do_all[rows, lanes], o[rows, lanes]
            kp, vp = k[:, lanes], v[:, lanes]
            turned = (dop.astype(F32) * op.astype(F32)).T
            pos = (lax.broadcasted_iota(jnp.int32, (1, BQ), 1) + i * BQ + 1).astype(F32)
            bound = jnp.maximum(pos, prefix)
            key_pos = lax.broadcasted_iota(jnp.int32, (LEN, 1), 0).astype(F32)
            seen = key_pos < bound
            dq_t = []
            for e in (0, 1):
                lit = head_lanes(BQ, e)
                qe = jnp.where(lit, qp, jnp.zeros_like(qp))
                de = jnp.where(lit, dop, jnp.zeros_like(dop))
                level = lse[2 * h + e, 0:1, pl.ds(pl.multiple_of(i * BQ, BQ), BQ)]
                inner_sum = jnp.sum(turned[e * HEAD : (e + 1) * HEAD], axis=0, keepdims=True)
                logits = dot(kp, qe, 1, 1)
                probs = jnp.where(seen, jnp.exp2(logits * SCALE2 - level), 0.0)
                slope = dot(vp, de, 1, 1)
                dlog = (probs * (slope - inner_sum)).astype(BF16)
                dv_acc[...] += dot(probs.astype(BF16), de)
                dk_acc[...] += dot(dlog, qe)
                dq_t.append(dot(k_turn[e * HEAD : (e + 1) * HEAD, :], dlog))
            dq_buf[h, rows, :] = (jnp.concatenate(dq_t, axis=0).T * SCALE).astype(BF16)
            launch(*g_copy(0, h, i))
            return inner

        lax.fori_loop(0, p.nq, query_step, 0)
        dkv_buf[0, h] = (dk_acc[...] * SCALE).astype(BF16)
        dkv_buf[1, h] = dv_acc[...].astype(BF16)

        def send(i, inner):
            launch(*g_copy(1, h, i))
            launch(*g_copy(2, h, i))
            return inner

        lax.fori_loop(0, p.nq, send, 0)
        return carry

    lax.fori_loop(0, p.pairs, pair_step, 0)

    for m in range(p.M):
        for g in range(p.groups):
            sent(*do_copy(m, g))

    def g_sent(i, carry):
        for part in range(3):
            for h in range(p.pairs):
                sent(*g_copy(part, h, i))
        return carry

    lax.fori_loop(0, p.nq, g_sent, 0)
    every = p.groups * p.pairs
    for part in range(3):
        for m in range(p.M):
            for piece in range(p.pieces):

                def got(n, carry):
                    lanes = pl.ds(pl.multiple_of(part * p.D + n * PAIR, PAIR), PAIR)
                    dst = home_out.at[m, pl.ds(piece * BQ, BQ), lanes]
                    pltpu.make_async_copy(dst, dst, g_rs.at[part, m, n, piece]).wait()
                    return carry

                lax.fori_loop(0, every, got, 0)


def back(plan, q, k, v, o, lse, preu, do_home):
    p = plan
    vmem = pl.BlockSpec(memory_space=pltpu.VMEM)
    dma = pltpu.SemaphoreType.DMA
    return pl.pallas_call(
        functools.partial(back_kernel, p),
        out_shape=jax.ShapeDtypeStruct((p.M, p.T, 3 * p.D), BF16),
        in_specs=[vmem] * 7,
        out_specs=vmem,
        scratch_shapes=[
            pltpu.VMEM((LEN, p.W), BF16),
            pltpu.VMEM((p.pairs, LEN, PAIR), BF16),
            pltpu.VMEM((2, p.pairs, LEN, PAIR), BF16),
            pltpu.VMEM((LEN, PAIR), F32),
            pltpu.VMEM((LEN, PAIR), F32),
            pltpu.VMEM((PAIR, LEN), BF16),
            dma((p.M, p.groups)), dma((p.P,)),
            dma((3, p.pairs, p.nq)), dma((3, p.M, p.groups * p.pairs, p.pieces)),
        ],
        compiler_params=pltpu.CompilerParams(
            collective_id=1, has_side_effects=True, vmem_limit_bytes=VMEM_LIMIT
        ),
        name="back",
    )(q, k, v, o, lse, preu, do_home)


def sum_kernel(plan, planes, nw, *refs):
    p = plan
    here = Place(p)
    s, c = here.s, here.c
    g = refs[:nw]
    small = refs[nw]
    outs = refs[nw + 1 : 2 * nw + 1]
    small_out = refs[2 * nw + 1]
    rest = refs[2 * nw + 2 :]
    held, mate, came, cross = rest[:nw], rest[nw : 2 * nw], rest[2 * nw : 3 * nw], rest[3 * nw : 4 * nw]
    small_in, small_all, ld, cx_s, cx_r, r_s, r_r, x_s, x_r, f_s, f_r, ss_s, ss_r, sa_s, sa_r = rest[4 * nw :]
    steps = p.S - 1
    plane = here.r // CORES

    peers = plane_peers(here) + [
        (s, lax.rem(plane + k, planes) * CORES + j) for k in range(1, planes) for j in range(CORES)
    ]
    greet(peers)

    loads, swaps = [], []
    for w in range(nw):
        loads.append(pltpu.make_async_copy(g[w].at[:, c], held[w], ld.at[w]))
        swaps.append(remote(g[w].at[:, 1 - c], mate[w], cx_s.at[w], cx_r.at[w], s, here.mate))
        swaps[-1].start()
        loads[-1].start()

    small_in[0] = small[s]
    tiny = []
    for k in range(1, p.S):
        to = lax.rem(s + k, p.S)
        tiny.append(remote(small.at[to], small_in.at[k], ss_s.at[k], ss_r.at[k], to, here.r))
        tiny[-1].start()

    ahead = [here.from_ring(lax.rem(here.ring + (1 if d == 0 else p.S - 1), p.S)) for d in (0, 1)]

    def target(d, t):
        i = lax.rem(here.ring + (2 * p.S - 1 - t if d == 0 else 1 + t), p.S)
        return here.from_ring(i)

    def part_rows(w, d):
        n = held[w].shape[1] // 2
        return pl.ds(d * n, n)

    def ring(w, d, t, to):
        return remote(
            held[w].at[to, part_rows(w, d), :], came[w].at[d, t], r_s.at[w, d, t], r_r.at[w, d, t], ahead[d], here.r
        )

    for w in range(nw):
        loads[w].wait()
        swaps[w].wait_recv()
        for d in (0, 1):
            to = target(d, 0)
            rows = part_rows(w, d)
            held[w][to, rows, :] = (held[w][to, rows, :].astype(F32) + mate[w][to, rows, :].astype(F32)).astype(BF16)
            ring(w, d, 0, to).start()

    def step(t, carry):
        for w in range(nw):
            for d in (0, 1):
                to = target(d, t)
                rows = part_rows(w, d)
                ring(w, d, t - 1, to).wait_recv()
                held[w][to, rows, :] = (
                    held[w][to, rows, :].astype(F32)
                    + mate[w][to, rows, :].astype(F32)
                    + came[w][d, t - 1].astype(F32)
                ).astype(BF16)

                @pl.when(t < steps)
                def _():
                    ring(w, d, jnp.minimum(t, steps - 1), to).start()

        return carry

    lax.fori_loop(1, steps + 1, step, 0)

    def over(w, k):
        to = lax.rem(plane + k, planes) * CORES + c
        return remote(held[w].at[s], cross[w].at[plane], x_s.at[w, k], x_r.at[w, plane], s, to)

    for w in range(nw):
        for k in range(1, planes):
            over(w, k).start()
        cross[w][plane] = held[w][s]

    for k in range(1, p.S):
        tiny[k - 1].wait_recv()
    total = small_in[0]
    for k in range(1, p.S):
        total = total + small_in[k]
    small_all[here.r] = total
    every = []
    for k in range(1, p.R):
        to = lax.rem(here.r + k, p.R)
        every.append(remote(small_all.at[here.r], small_all.at[here.r], sa_s.at[k], sa_r.at[here.r], s, to))
        every[-1].start()

    hand = []
    for w in range(nw):
        for k in range(1, planes):
            off = lax.rem(plane + k, planes)
            remote(held[w].at[s], cross[w].at[off], x_s.at[w, k], x_r.at[w, off], s, here.r).wait_recv()
        sum_ = cross[w][0].astype(F32)
        for k in range(1, planes):
            sum_ = sum_ + cross[w][k].astype(F32)
        half = outs[w].at[c]
        half[...] = sum_.astype(BF16)
        hand.append(remote(half, half, f_s.at[w], f_r.at[w], s, here.mate))
        hand[-1].start()

    for k in range(1, p.R):
        off = lax.rem(here.r + k, p.R)
        remote(small_all.at[0], small_all.at[off], sa_s.at[k], sa_r.at[off], s, here.r).wait_recv()
    total = small_all[0]
    for k in range(1, p.R):
        total = total + small_all[k]
    small_out[...] = total

    for copy in swaps + tiny + every:
        copy.wait_send()
    for w in range(nw):
        for k in range(1, planes):
            over(w, k).wait_send()
        hand[w].wait_send()
        other = outs[w].at[1 - c]
        remote(other, other, f_s.at[w], f_r.at[w], s, here.mate).wait_recv()

    def drain(t, carry):
        for w in range(nw):
            for d in (0, 1):
                ring(w, d, t, target(d, t)).wait_send()
        return carry

    lax.fori_loop(0, steps, drain, 0)


def summed(plan, grads, small):
    p = plan
    nw = len(grads)
    planes = p.R // CORES
    steps = p.S - 1
    split = []
    for grad in grads:
        rows, cols = grad.shape
        split.append(grad.reshape(p.S, CORES, rows // (p.S * CORES), cols))
    any_space = pl.BlockSpec(memory_space=pl.ANY)
    vmem = pl.BlockSpec(memory_space=pltpu.VMEM)
    dma = pltpu.SemaphoreType.DMA
    shapes = [(h.shape[2], h.shape[3]) for h in split]
    outs = pl.pallas_call(
        functools.partial(sum_kernel, p, planes, nw),
        out_shape=[jax.ShapeDtypeStruct((CORES,) + sh, BF16) for sh in shapes]
        + [jax.ShapeDtypeStruct(small.shape[1:], F32)],
        in_specs=[any_space] * nw + [vmem],
        out_specs=[vmem] * (nw + 1),
        scratch_shapes=[pltpu.VMEM((p.S,) + sh, BF16) for sh in shapes]
        + [pltpu.VMEM((p.S,) + sh, BF16) for sh in shapes]
        + [pltpu.VMEM((2, steps, sh[0] // 2, sh[1]), BF16) for sh in shapes]
        + [pltpu.VMEM((planes,) + sh, BF16) for sh in shapes]
        + [
            pltpu.VMEM(small.shape, F32),
            pltpu.VMEM((p.R,) + small.shape[1:], F32),
            dma((nw,)), dma((nw,)), dma((nw,)),
            dma((nw, 2, steps)), dma((nw, 2, steps)),
            dma((nw, planes)), dma((nw, planes)),
            dma((nw,)), dma((nw,)),
            dma((p.S,)), dma((p.S,)), dma((p.R,)), dma((p.R,)),
        ],
        compiler_params=pltpu.CompilerParams(
            collective_id=2, has_side_effects=True, vmem_limit_bytes=VMEM_LIMIT
        ),
        name="sums",
    )(*split, small)
    full = [o.reshape(CORES * o.shape[1], o.shape[2]).astype(F32) for o in outs[:nw]]
    return full, outs[nw]


def smooth(values):
    return jax.nn.gelu(values, approximate=False)


def per_device(
    sizes,
    inputs,
    prefix,
    qkv_weight,
    qv_bias,
    out_weight,
    branch_bias,
    up_weight,
    up_bias,
    down_weight,
    norm_gain,
    norm_bias,
    cotangent,
):
    p = Plan(sizes, (inputs.shape[0], 1, inputs.shape[2], inputs.shape[3]))
    tokens_all = p.M * p.T
    x = inputs[:, 0]
    width = p.D // p.S
    spare = max(128 - width, 0)
    par = jnp.concatenate([qv_bias, branch_bias, norm_gain, norm_bias, up_bias.reshape(-1, width)], axis=0)
    par = jnp.pad(par, ((0, 0), (0, spare)))
    pre = jnp.broadcast_to(prefix[:, 0].reshape(-1, 1).astype(F32), (p.M * p.Q, 128))
    pre = jnp.pad(pre, ((0, 8 - p.M * p.Q), (0, 0)))
    (wq, wo, wu, wd, parf, a_home, q, k, v, o, lse, preu, o_home) = fore(
        p, x, par, pre, (qkv_weight, out_weight, up_weight, down_weight)
    )
    par32 = parf.astype(F32)
    bias_branch = par32[2:4]
    gains, shifts = par32[4:8], par32[8:12]
    bias_up = par32[12:].reshape(-1, p.S, width).transpose(1, 0, 2).reshape(-1)

    tokens = x.reshape(tokens_all, p.D).astype(F32)
    upstream = cotangent[:, 0].reshape(tokens_all, p.D).astype(F32)
    mixed_low = o_home.reshape(tokens_all, p.D)
    a_low = a_home.reshape(tokens_all, p.D)
    branch = dot(mixed_low, wo) + bias_branch[0]
    side, pull_side = jax.vjp(normed, branch, gains[1:2], shifts[1:2])
    stream = tokens + side
    normal_mid, pull_mid = jax.vjp(normed, stream, gains[2:3], shifts[2:3])
    middle_low = normal_mid.astype(BF16)
    upper = dot(middle_low, wu) + bias_up
    active, pull_active = jax.vjp(smooth, upper)
    active_low = active.astype(BF16)
    lower = dot(active_low, wd) + bias_branch[1]
    closing, pull_close = jax.vjp(normed, lower, gains[3:4], shifts[3:4])
    output = (stream + closing).astype(BF16)
    grad_lower, gain_three, shift_three = pull_close(upstream)
    lower_low = grad_lower.astype(BF16)
    grad_active = dot(lower_low, wd, 1, 1)
    (grad_upper,) = pull_active(grad_active)
    upper_low = grad_upper.astype(BF16)
    grad_middle = dot(upper_low, wu, 1, 1)
    grad_mid_in, gain_two, shift_two = pull_mid(grad_middle)
    grad_stream = grad_mid_in + upstream
    grad_branch, gain_one, shift_one = pull_side(grad_stream)
    branch_low = grad_branch.astype(BF16)
    grad_mixed = dot(branch_low, wo, 1, 1).astype(BF16)

    joined = back(p, q, k, v, o, lse, preu, grad_mixed.reshape(p.M, p.T, p.D))
    joined_low = joined.reshape(tokens_all, 3 * p.D)
    grad_normal = dot(joined_low, wq, 1, 1)
    _, pull_in = jax.vjp(normed, tokens, gains[0:1], shifts[0:1])
    grad_tokens, gain_zero, shift_zero = pull_in(grad_normal)
    input_grad = (grad_stream + grad_tokens).astype(BF16)

    def column_sum(values):
        return jnp.sum(values.astype(F32), axis=0, keepdims=True)

    du_sum = column_sum(upper_low).reshape(p.S, -1, width).transpose(1, 0, 2).reshape(-1, p.D)
    joined_sum = column_sum(joined_low)
    small = jnp.concatenate(
        [
            joined_sum[:, : p.D], joined_sum[:, 2 * p.D :],
            column_sum(branch_low), column_sum(lower_low),
            gain_zero, gain_one, gain_two, gain_three,
            shift_zero, shift_one, shift_two, shift_three,
            du_sum,
        ], axis=0,
    )
    small = jnp.pad(small.reshape(-1, p.S, width).transpose(1, 0, 2), ((0, 0), (0, 0), (0, spare)))
    grads = (
        dot(a_low, joined_low, 0, 0).astype(BF16),
        dot(mixed_low, branch_low, 0, 0).astype(BF16),
        dot(middle_low, upper_low, 0, 0).astype(BF16),
        dot(active_low, lower_low, 0, 0).astype(BF16),
    )
    full, tiny = summed(p, grads, small)
    tiny = tiny[:, :width]
    shaped = (p.M, 1, p.T, p.D)
    return (
        output.reshape(shaped),
        input_grad.reshape(shaped),
        full[0],
        tiny[0:2],
        full[1],
        tiny[2:4],
        full[2],
        tiny[12:].reshape(-1),
        full[3],
        tiny[4:8],
        tiny[8:12],
    )


def solution(mesh):
    sizes = {name: mesh.shape[name] for name in ("shard", "replica")}
    placed = (
        P(None, "replica", "shard", None),
        P(None, "replica", None),
        P("shard", None),
        P(None, "shard"),
        P("shard", None),
        P(None, "shard"),
        P("shard", None),
        P("shard"),
        P("shard", None),
        P(None, "shard"),
        P(None, "shard"),
        P(None, "replica", "shard", None),
    )
    return jax.shard_map(
        functools.partial(per_device, sizes),
        mesh=mesh,
        in_specs=placed,
        out_specs=(
            P(None, "replica", "shard", None),
            P(None, "replica", "shard", None),
            P("shard", None),
            P(None, "shard"),
            P("shard", None),
            P(None, "shard"),
            P("shard", None),
            P("shard"),
            P("shard", None),
            P(None, "shard"),
            P(None, "shard"),
        ),
        check_vma=False,
    )
```

time: 2100 us -> 638 us (0.30)
  waiting for transfers between devices: 1400 us -> 0 us
  Pallas kernels: 0 us -> 494 us
  matrix products: 328 us -> 100 us
  blocking collectives: 128 us -> 0 us
  local copies, waits for them, and re-layouts: 127 us -> 13.7 us
  other arithmetic: 82.3 us -> 19.5 us
    reduce_scatter x8 -> x0, waiting for transfers between devices: 661 us -> none  [the longest x1 152 us: per_device(): lax.psum_scatter(running[4].astype(jnp.bfloat16), 'shard', scatter_dimens...]
    pallas_call x0 -> x3, Pallas kernels: none -> 494 us  [the longest x1 201 us: fore(): pl.pallas_call(functools.partial(fore_kernel, p), out_shape=out_shape, in...]
    all_gather x8 -> x0, waiting for transfers between devices: 448 us -> none  [the longest x2 135 us: per_device(): keys_group = lax.all_gather(keys_own, 'shard', axis=0, tiled=True)]
    unnamed x25 -> x0, waiting for transfers between devices: 229 us -> none
    dot_general x80 -> x11, matrix products: 328 us -> 100 us  [dot(): lax.dot_general(a, b, (((ca,), (cb,)), ((), ())), preferred_element_type=...]
    all_gather x5 -> x0, blocking collectives: 102 us -> none  [the longest x1 26.5 us: per_device(): upbias_full = lax.all_gather(up_bias, 'shard', axis=0, tiled=True)]
    psum x1 -> x0, waiting for transfers between devices: 61.3 us -> none  [per_device(): lax.psum(running[0].astype(jnp.bfloat16), 'replica').astype(jnp.float32)]
    dynamic_slice x72 -> x0, local copies, waits for them, and re-layouts: 52.6 us -> none  [the longest x56 43.1 us: column_slice(): return lax.dynamic_slice_in_dim(matrix, column_start, column_count, 1)]
  transfers between devices with their start and end apart: 21 -> 0, of which waited for: 20 -> 0; matrix products, arithmetic and copies ran while one was open for 16% -> 0% of each run, Pallas kernels for 0% -> 0%
where the time goes in v1:
time: 638 us; the launch traced here: 629 us
  Pallas kernels  494 us (77%)
  matrix products  100 us (16%)
  other arithmetic  19.5 us (3%)
  local copies, waits for them, and re-layouts  13.7 us (2%)
    pallas_call x1, Pallas kernels, fore(): pl.pallas_call(functools.partial(fore_kernel, p), out_shape=out_shape, in...  201 us
    pallas_call x1, Pallas kernels, summed(): pl.pallas_call(functools.partial(sum_kernel, p, planes, nw), out_shape=[j...  176 us
    pallas_call x1, Pallas kernels, back(): pl.pallas_call(functools.partial(back_kernel, p), out_shape=jax.ShapeDtyp...  116 us
    dot_general x11, matrix products, dot(): lax.dot_general(a, b, (((ca,), (cb,)), ((), ())), preferred_element_type=...  100 us

profile of v1, /device:TPU:0, one launch (start us, length us, event | category | flops | bytes accessed | tf_op | source)
XLA Modules:
  0.0 628.8 jit_solution(7098717657113511668)
XLA Ops:
  0.6 2.6 concatenate.31.par
  4.6 201.3 %fore.1 = (bf16[1024,3072]{1,0:T(8,128)(2,1)}, bf16[1024,1024]{1,0:T(8,128)(2,1)}, bf16[1024,4096]{1,0:T(8,128)(2,1)}, bf16[4096,1024]{1,0:T(8,128)(2,1)}, bf16[...) custom-call(bf16[2,256,1024]{2,1,0:T(8,128)(2,1)} %bitcast.130, ...), custom_call_target="tpu_custom_call" | custom-call | tf_op jit(solution)/shard_map/fore/pallas_call | solution.py:415
  205.8 1.0 fusion.30
  207.5 3.4 add_reduce_fusion.1
  211.4 0.8 copy-done
  212.2 0.8 fusion.29
  213.4 26.1 %multiply_convert_fusion = (bf16[512,4096]{1,0:T(8,128)(2,1)S(1)}, f32[512,4096]{1,0:T(8,128)}, f32[512,4096]{1,0:T(8,128)}) fusion(f32[4096]{0:T(1024)S(1)} %bitcast.170, bf16[1024,4096]{1,0:T(8,128)(2,1)S(1)} %bitcast.185, f32[512,1024]{1,0:T(8,128)S(1)} %get-tuple-element.97, f32[1024]{0:T(1024)S(1)} %bitcast.178, f32[1024]{0:T(1024)S(1)} %bitcast.173, ...), kind=kOutput, calls=%fused_computation.5 | convolution fusion | flops 4436000768 | bytes 31485952 | tf_op jit(solution)/shard_map/dot_general | solution.py:118
  239.6 4.7 add_reduce_fusion
  244.7 0.8 copy-done.6
  245.5 0.9 fusion.9
  246.4 2.0 fusion.27
  248.7 13.8 %convert_reduce_fusion = (f32[4096]{0:T(1024)S(1)}, bf16[512,4096]{1,0:T(8,128)(2,1)S(1)}) fusion(f32[512,4096]{1,0:T(8,128)} %get-tuple-element.95, f32[512,4096]{1,0:T(8,128)} %get-tuple-element.121, f32[4096]{0:T(1024)S(1)} %bitcast.171, bf16[512,1024]{1,0:T(8,128)(2,1)S(1)} %get-tuple-element.84, bf16[4096,1024]{1,0:T(8,128)(2,1)} %get-tuple-element.33), kind=kOutput, calls=%fused_computation.3 | convolution fusion | flops 4330614784 | bytes 30441472 | tf_op jit(solution)/shard_map/dot_general | solution.py:118
  262.5 20.2 %multiply_reduce_fusion = (f32[1024]{0:T(1024)S(1)}, f32[512]{0:T(512)S(1)}, f32[1024]{0:T(1024)S(1)}, f32[512,1024]{1,0:T(8,128)S(1)}) fusion(f32[512,1024]{1,0:T(8,128)S(1)} %get-tuple-element.97, f32[512]{0:T(512)S(1)} %fusion.19, f32[512]{0:T(512)S(1)} %broadcast_multiply_fusion.2, f32[1024]{0:T(1024)S(1)} %bitcast.174, ...), kind=kOutput, calls=%fused_computation.46 | convolution fusion | flops 4299159040 | bytes 16795648 | tf_op jit(solution)/shard_map/dot_general | solution.py:118
  283.5 1.1 multiply_reduce_fusion.1
  284.8 0.8 fusion.25
  286.2 1.7 copy-done.17
  287.8 2.3 convolution_convert_fusion.3
  290.1 116.3 %back.1 = bf16[2,256,3072]{2,1,0:T(8,128)(2,1)} custom-call(bf16[2048,256]{1,0:T(8,128)(2,1)} %get-tuple-element.34.q, bf16[2048,256]{1,0:T(8,128)(2,1)} %get-tuple-element.35.k, bf16[2048,256]{1,0:T(8,128)(2,1)} %get-tuple-element.36.v, bf16[2048,256]{1,0:T(8,128)(2,1)} %get-tuple-element.37.o, f32[4,8,2048]{2,1,0:T(8,128)} %get-tuple-element.38.lse, ...), custom_call_target="tpu_custom_call" | custom-call | tf_op jit(solution)/shard_map/back/pallas_call | solution.py:560
  406.4 7.7 %fusion.24 = (f32[1024]{0:T(1024)S(1)}, f32[512]{0:T(512)S(1)}, f32[512,1024]{1,0:T(8,128)S(1)}) fusion(f32[1024]{0:T(1024)S(1)} %bitcast.154, f32[512]{0:T(512)S(1)} %bitcast.158, bf16[2,1,256,1024]{3,2,1,0:T(8,128)(2,1)} %param.12, bf16[512,3072]{1,0:T(8,128)(2,1)} %bitcast.131, bf16[1024,3072]{1,0:T(8,128)(2,1)} %get-tuple-element.40), kind=kOutput, calls=%fused_computation.96 | convolution fusion | flops 3224369664 | bytes 12595200 | tf_op jit(solution)/shard_map/dot_general | solution.py:118
  414.5 1.0 fusion.15
  415.7 1.7 add_convert_fusion.1
  418.2 5.5 bitcast_convert_fusion
  423.7 2.6 convolution_convert_fusion.2
  426.4 0.9 copy-done.23
  427.3 7.5 %convolution_convert_fusion.1 = bf16[1024,4096]{1,0:T(8,128)(2,1)} fusion(bf16[512,4096]{1,0:T(8,128)(2,1)S(1)} %copy-done.23, f32[512,1024]{1,0:T(8,128)S(1)} %copy-done.3, f32[1024]{0:T(1024)S(1)} %bitcast.179, f32[1024]{0:T(1024)S(1)} %bitcast.176, f32[512]{0:T(512)S(1)} %fusion.19, f32[512]{0:T(512)S(1)} %broadcast_multiply_fusion.2), kind=kOutput, calls=%fused_computation.20 | convolution fusion | flops 4301783040 | bytes 14692352 | tf_op jit(solution)/shard_map/dot_general | solution.py:118
  434.8 6.8 %convolution_convert_fusion = bf16[4096,1024]{1,0:T(8,128)(2,1)} fusion(bf16[512,4096]{1,0:T(8,128)(2,1)S(1)} %copy-done.21, bf16[512,1024]{1,0:T(8,128)(2,1)S(1)} %copy-done.12), kind=kOutput, calls=%fused_computation.19 | convolution fusion | flops 4299161600 | bytes 13631488 | tf_op jit(solution)/shard_map/dot_general | solution.py:118
  443.0 1.3 concatenate.44
  444.3 176.3 %sums.1 = (bf16[2,64,3072]{2,1,0:T(8,128)(2,1)}, bf16[2,64,1024]{2,1,0:T(8,128)(2,1)}, bf16[2,64,4096]{2,1,0:T(8,128)(2,1)}, bf16[2,256,1024]{2,1,0:T(8,128)(2,1)}, f32[16,128]{1,0:T(8,128)}) custom-call(bf16[8,2,64,3072]{3,2,1,0:T(8,128)(2,1)} %bitcast.134, bf16[8,2,64,1024]{3,2,1,0:T(8,128)(2,1)} %bitcast.135, bf16[8,2,64,4096]{3,2,1,0:T(8,128)(2,1)} %bitcast.132, ...), custom_call_target="tpu_custom_call" | custom-call | tf_op jit(solution)/shard_map/sums/pallas_call | solution.py:732
  620.6 2.5 bitcast_convert_fusion.3
  623.8 0.9 bitcast_convert_fusion.4
  624.6 1.6 bitcast_convert_fusion.2
  626.8 1.6 bitcast_convert_fusion.1
  (89 shorter events, 9.2 us)
Async XLA Ops:
  207.5 5.8 slice-start
  210.9 1.2 copy-start
  210.9 2.5 slice-start.1
  212.1 27.4 %slice-start.2 = ((s8[8388608]{0:T(1024)(128)(4,1)}), s8[4194304]{0:T(1024)(128)(4,1)S(1)}, s32[]{:S(2)}) async-start(s8[8388608]{0:T(1024)(128)(4,1)} %bitcast.186), calls=%async_computation.2 | async-start | bytes 8388608
  212.9 69.8 %copy-start.2 = (f32[512,1024]{1,0:T(8,128)}, f32[512,1024]{1,0:T(8,128)S(1)}, u32[]{:S(2)}) copy-start(f32[512,1024]{1,0:T(8,128)S(1)} %get-tuple-element.97) | copy-start | bytes 6291460
  213.4 26.1 %slice-start.3 = ((s8[8388608]{0:T(1024)(128)(4,1)}), s8[4194304]{0:T(1024)(128)(4,1)S(1)}, s32[]{:S(2)}) async-start(s8[8388608]{0:T(1024)(128)(4,1)} %bitcast.186), calls=%async_computation.3 | async-start | bytes 8388608
  239.5 4.7 copy-start.20
  244.2 1.2 copy-start.6
  248.7 13.8 %copy-start.11 = (bf16[512,1024]{1,0:T(8,128)(2,1)}, bf16[512,1024]{1,0:T(8,128)(2,1)S(1)}, u32[]{:S(2)}) copy-start(bf16[512,1024]{1,0:T(8,128)(2,1)S(1)} %get-tuple-element.84) | copy-start | bytes 3145732
  262.4 20.3 %copy-start.22 = (bf16[512,4096]{1,0:T(8,128)(2,1)}, bf16[512,4096]{1,0:T(8,128)(2,1)S(1)}, u32[]{:S(2)}) copy-start(bf16[512,4096]{1,0:T(8,128)(2,1)S(1)} %get-tuple-element.82) | copy-start | bytes 12582916
  284.6 1.3 copy-start.4
  285.9 2.0 copy-start.17
  286.1 4.0 copy-start.13
  406.4 7.7 %copy-start.1 = (bf16[2,1,256,1024]{3,2,1,0:T(8,128)(2,1)S(1)}, bf16[2,1,256,1024]{3,2,1,0:T(8,128)(2,1)}, u32[]{:S(2)}) copy-start(bf16[2,1,256,1024]{3,2,1,0:T(8,128)(2,1)} %param.12) | copy-start | bytes 3145732
  414.1 1.6 copy-start.5
  415.7 2.3 copy-start.8
  415.7 2.5 copy-start.19
  418.2 5.5 copy-start.14
  418.2 5.5 copy-start.18
  423.7 2.6 copy-start.3
  423.7 3.6 copy-start.23
  427.3 7.5 %copy-start.12 = (bf16[512,1024]{1,0:T(8,128)(2,1)S(1)}, bf16[512,1024]{1,0:T(8,128)(2,1)}, u32[]{:S(2)}) copy-start(bf16[512,1024]{1,0:T(8,128)(2,1)} %copy-done.11) | copy-start | bytes 3145732
  427.3 7.5 %copy-start.21 = (bf16[512,4096]{1,0:T(8,128)(2,1)S(1)}, bf16[512,4096]{1,0:T(8,128)(2,1)}, u32[]{:S(2)}) copy-start(bf16[512,4096]{1,0:T(8,128)(2,1)} %copy-done.20) | copy-start | bytes 12582916
  441.6 1.2 copy-start.7
  620.6 2.6 copy-start.16
  620.6 3.1 copy-start.15
  620.6 4.0 copy-start.10
  623.2 3.6 copy-start.9

commit v2 on v1

v2 whole, which is shorter than its diff:
```python
import functools
import math

import jax
import jax.numpy as jnp
from jax import lax
from jax.experimental import pallas as pl
from jax.experimental.pallas import tpu as pltpu
from jax.sharding import PartitionSpec as P

HEAD = 64
LEN = 2048
CORES = 2
PAIR = 2 * HEAD
BQ = 256
EPS = 1e-05
MASKED = -1e30
SCALE = HEAD ** (-0.5)
SCALE2 = SCALE * math.log2(math.e)
F32 = jnp.float32
BF16 = jnp.bfloat16
MESH = pl.DeviceIdType.MESH
VMEM_LIMIT = 66_000_000
LAG = 2
KEYS = 512
SIDE_FIRST = (False, True, True)
SUM_LAG = 2
COLUMN_FIRST = (True, True, True, False)


class Plan:
    def __init__(self, mesh_shape, inputs_shape):
        self.S = mesh_shape["shard"]
        self.R = mesh_shape["replica"]
        self.M, _, self.T, self.D = inputs_shape
        self.Q = self.T * self.S // LEN
        self.P = LEN // self.T
        self.U = self.M * self.Q * CORES
        self.cpu = self.S // self.U
        self.heads = self.D // HEAD
        self.W = self.D // (CORES * self.cpu)
        self.pairs = self.W // PAIR
        self.groups = CORES * self.cpu
        self.pieces = self.T // BQ
        self.nq = LEN // BQ
        self.near = self.P // self.cpu
        self.width = self.D // self.S
        assert self.cpu == 2 and self.pairs == 2 and self.T % BQ == 0 and LEN % self.T == 0


class Place:
    def __init__(self, plan):
        self.p = plan
        self.s = lax.axis_index("shard")
        self.r = lax.axis_index("replica")
        self.c = lax.rem(self.r, CORES)
        self.chip = self.r - self.c
        self.mate = self.chip + (1 - self.c)
        self.unit = self.s // plan.cpu
        self.lane = lax.rem(self.s, plan.cpu)
        self.group = self.c * plan.cpu + self.lane
        self.uc = lax.rem(self.unit, CORES)
        self.um = lax.rem(self.unit // CORES, plan.M)
        self.uq = self.unit // (CORES * plan.M)
        self.ring = self.to_ring(self.s)
        self.plane = self.r // CORES
        self.side = lax.rem(self.plane, 2)
        self.twin = self.r + CORES * (1 - 2 * self.side)
        self.row = self.s // 2
        self.col = lax.rem(self.s, 2)
        self.beside = 2 * self.row + 1 - self.col
        self.rows = plan.S // 2

    def unit_of(self, c, m, s):
        return ((s // self.p.P) * self.p.M + m) * CORES + c

    def to_ring(self, s):
        half = self.p.S // 2
        row, col = s // 2, lax.rem(s, 2)
        return row + col * (2 * half - 1 - 2 * row)

    def from_ring(self, i):
        n = self.p.S
        return jnp.where(i < n // 2, 2 * i, 2 * (n - 1 - i) + 1)


def remote(src, dst, send, recv, s, r):
    return pltpu.make_async_remote_copy(
        src_ref=src, dst_ref=dst, send_sem=send, recv_sem=recv, device_id=(s, r), device_id_type=MESH
    )


def launch(away, far, near):
    @pl.when(away)
    def _():
        far().start()

    @pl.when(jnp.logical_not(away))
    def _():
        pltpu.make_async_copy(*near).start()


def sent(away, far, near):
    @pl.when(away)
    def _():
        far().wait_send()


def greet(peers):
    barrier = pltpu.get_barrier_semaphore()
    for s, r in peers:
        pl.semaphore_signal(barrier, inc=1, device_id=(s, r), device_id_type=MESH)
    pl.semaphore_wait(barrier, len(peers))


def plane_peers(here):
    n = here.p.S * CORES
    own = here.s * CORES + here.c
    out = []
    for k in range(1, n):
        i = lax.rem(own + k, n)
        out.append((i // CORES, here.chip + lax.rem(i, CORES)))
    return out


def normed(values, gain, shift):
    centre = values - jnp.mean(values, axis=-1, keepdims=True)
    spread = jnp.mean(centre * centre, axis=-1, keepdims=True)
    return centre * lax.rsqrt(spread + EPS) * gain + shift


def dot(a, b, ca=1, cb=0):
    return lax.dot_general(a, b, (((ca,), (cb,)), ((), ())), preferred_element_type=F32)


def head_lanes(rows, which):
    lane = lax.broadcasted_iota(jnp.int32, (rows, PAIR), 1)
    return (lane < HEAD) if which == 0 else (lane >= HEAD)


def fore_kernel(
    plan, x, par, pre, wq, wo, wu, wd,
    wqf, wof, wuf, wdf, parf, ah, q_out, k_out, v_out, o_out, lse_out, preu, oh, a_all, wcol,
    parg, pre2,
    par_ss, par_rs, pre_sem, loc_sem, a_ss, a_rs, af_ss, z_ss, z_rs, wa_ss, wa_rs, wb_ss, wb_rs, wm_ss, wm_rs,
    o_ss, o_rs, col_sem,
):
    p = plan
    here = Place(p)
    s, c = here.s, here.c
    mine, full = (wq, wo, wu, wd), (wqf, wof, wuf, wdf)
    nw = len(mine)
    first = COLUMN_FIRST
    greet(plane_peers(here) + [(s, here.twin)])

    parg[s] = par[...]
    small = []
    for k in range(1, p.S):
        to = lax.rem(s + k, p.S)
        small.append(remote(par, parg.at[s], par_ss.at[k], par_rs.at[k], to, here.r))
        small[-1].start()
    swap = remote(pre, pre2, pre_sem.at[0], pre_sem.at[1], s, here.mate)
    swap.start()

    z, nz = here.row, here.rows

    def where(w, zr, fa, fb, core):
        fy, fx = (fa, fb) if first[w] else (fb, fa)
        col = here.col if fy == 0 else 1 - here.col
        side = here.side if fx == 0 else 1 - here.side
        n, width = mine[w].shape[0], mine[w].shape[1] // 2
        rows = pl.ds(pl.multiple_of((2 * zr + col) * n + core * (n // 2), n // 2), n // 2)
        return full[w].at[rows, pl.ds(pl.multiple_of(side * width, width), width)]

    def origin(w, fa):
        n, width = mine[w].shape[0], mine[w].shape[1] // 2
        side = here.side if fa == 0 else 1 - here.side
        rows = pl.ds(pl.multiple_of(c * (n // 2), n // 2), n // 2)
        return mine[w].at[rows, pl.ds(pl.multiple_of(side * width, width), width)]

    def peer(w, second):
        return (here.beside, here.r) if first[w] == (second == 0) else (s, here.twin)

    def z_send(w, d, k):
        sign = 1 - 2 * d
        part = where(w, z - sign * (k - 1), 0, 0, c)
        src = origin(w, 0) if isinstance(k, int) and k == 1 else part
        return remote(src, part, z_ss.at[w, d, k - 1], z_rs.at[w, d, k - 1], s + 2 * sign, here.r)

    def z_came(w, d, k):
        sign = 1 - 2 * d
        part = where(w, z - sign * k, 0, 0, c)
        return remote(part, part, z_ss.at[w, d, k - 1], z_rs.at[w, d, k - 1], s, here.r)

    def to_first(w, zr, src=None):
        part = where(w, zr, 0, 0, c)
        return remote(part if src is None else src, part, wa_ss.at[w, zr], wa_rs.at[w, zr], *peer(w, 0))

    def to_second(w, fa, zr, src=None):
        part = where(w, zr, fa, 0, c)
        return remote(part if src is None else src, part, wb_ss.at[w, fa, zr], wb_rs.at[w, fa, zr], *peer(w, 1))

    def to_mate(w, fa, fb, zr, core):
        part = where(w, zr, fa, fb, core)
        at = 2 * fa + fb
        return remote(part, part, wm_ss.at[w, at, zr], wm_rs.at[w, at, zr], s, here.mate)

    def first_came(w, zr):
        part = where(w, zr, 1, 0, c)
        return remote(part, part, wa_ss.at[w, zr], wa_rs.at[w, zr], s, here.r)

    def second_came(w, fa, zr):
        part = where(w, zr, fa, 1, c)
        return remote(part, part, wb_ss.at[w, fa, zr], wb_rs.at[w, fa, zr], s, here.r)

    def on_grid(d, k):
        return z >= k if d == 0 else z + k < nz

    def can_send(d):
        return z < nz - 1 if d == 0 else z > 0

    def gather_start(w):
        for d in (0, 1):

            @pl.when(can_send(d))
            def _():
                z_send(w, d, 1).start()

        if first[w]:
            to_first(w, z, origin(w, 0)).start()
        else:
            to_second(w, 0, z, origin(w, 0)).start()
            to_second(w, 1, z, origin(w, 1)).start()

    def gather_slot(w, k, lag):
        for d in (0, 1):
            sign = 1 - 2 * d

            @pl.when(jnp.logical_and(k >= 1, on_grid(d, k)))
            def _():
                at = jnp.maximum(k, 1)
                z_came(w, d, at).wait_recv()
                zr = z - sign * at

                @pl.when(can_send(d))
                def _():
                    z_send(w, d, at + 1).start()

                to_first(w, zr).start()
                to_second(w, 0, zr).start()
                to_mate(w, 0, 0, zr, c).start()

        def at_distance(j, least, body):
            for d in (0, 1):
                ok = jnp.logical_and(j >= max(least, d), on_grid(d, j))

                @pl.when(ok)
                def _():
                    body(z - (1 - 2 * d) * jnp.maximum(j, 0))

        def after_first(zr):
            first_came(w, zr).wait_recv()
            to_second(w, 1, zr).start()
            to_mate(w, 1, 0, zr, c).start()

        at_distance(k - 1, 0 if first[w] else 1, after_first)

        def after_second(fa):
            def body(zr):
                second_came(w, fa, zr).wait_recv()
                to_mate(w, fa, 1, zr, c).start()

            return body

        at_distance(k - 1 - lag, 1 if first[w] else 0, after_second(0))
        at_distance(k - 2 - lag, 0, after_second(1))

    def mate_pieces(w, zr, act):
        other = zr != z

        @pl.when(other)
        def _():
            act(0, 0)

        if first[w]:

            @pl.when(other)
            def _():
                act(0, 1)

            act(1, 0)
        else:

            @pl.when(other)
            def _():
                act(1, 0)

            act(0, 1)
        act(1, 1)

    def gather_wait(w):
        def one(zr, carry):
            mate_pieces(w, zr, lambda fa, fb: to_mate(w, fa, fb, zr, 1 - c).wait_recv())
            return carry

        lax.fori_loop(0, nz, one, 0)

    def gather_drain(w):
        def one(zr, carry):
            mate_pieces(w, zr, lambda fa, fb: to_mate(w, fa, fb, zr, c).wait_send())
            if first[w]:
                to_first(w, zr).wait_send()

                @pl.when(zr != z)
                def _():
                    to_second(w, 0, zr).wait_send()
            else:

                @pl.when(zr != z)
                def _():
                    to_first(w, zr).wait_send()

                to_second(w, 0, zr).wait_send()
            to_second(w, 1, zr).wait_send()
            for d in (0, 1):
                reach = zr <= z if d == 0 else zr < nz - z

                @pl.when(jnp.logical_and(can_send(d), reach))
                def _():
                    z_send(w, d, zr + 1).wait_send()

            return carry

        lax.fori_loop(0, nz, one, 0)

    gather_start(0)
    local = []
    for w in range(nw):
        n = mine[w].shape[0]
        local.append(
            pltpu.make_async_copy(mine[w], full[w].at[pl.ds(pl.multiple_of(s * n, n), n), :], loc_sem.at[w])
        )
        local[-1].start()

    for k in range(1, p.S):
        small[k - 1].wait_recv()
    parf[...] = jnp.concatenate([parg[k][:, : p.D // p.S] for k in range(p.S)], axis=1)
    gain = parf[4:5, :].astype(F32)
    shift = parf[8:9, :].astype(F32)
    rows_here = pl.ds(pl.multiple_of(lax.rem(s, p.P) * p.T, p.T), p.T)

    def first_hop(m):
        to = here.unit_of(c, m, s) * p.cpu + here.lane
        far = lambda: remote(ah.at[m], a_all.at[rows_here, :], a_ss.at[m], a_rs.at[lax.rem(s, p.P)], to, here.r)
        return to, far

    for m in range(p.M):
        ah[m] = normed(x[m].astype(F32), gain, shift).astype(BF16)
        to, far = first_hop(m)

        @pl.when(to != s)
        def _():
            far().start()

        @pl.when(to == s)
        def _():
            a_all[rows_here, :] = ah[m]

    primary = c == here.uc

    def a_rows(j):
        return pl.ds(pl.multiple_of(j * p.T, p.T), p.T)

    def a_forward(j, k):
        part = a_all.at[a_rows(j), :]
        if k == 0:
            return remote(part, part, af_ss.at[j, 0], a_rs.at[j], s, here.mate)
        to = here.unit * p.cpu + lax.rem(here.lane + k, p.cpu)
        return remote(part, part, af_ss.at[j, k], a_rs.at[j], to, here.r)

    def a_wait(j):
        part = a_all.at[a_rows(j), :]
        remote(part, part, af_ss.at[j, 0], a_rs.at[j], s, here.mate).wait_recv()

    near = p.near

    zi = here.unit - here.uq * near

    def a_at(k, body):
        for d in (0, 1):
            if k or not d:
                ok = zi >= k if d == 0 else zi + k < near

                @pl.when(jnp.logical_and(primary, ok))
                def _():
                    body(zi - (1 - 2 * d) * k)

    def a_near(jj):
        j = jj * p.cpu + here.lane

        @pl.when(here.uq * p.P + j != s)
        def _():
            a_wait(j)

        for k in list(range(1, p.cpu)) + [0]:
            a_forward(j, k).start()

    def a_far(jj):
        for k in range(1, p.cpu):
            j = jj * p.cpu + lax.rem(here.lane + k, p.cpu)
            a_wait(j)
            a_forward(j, 0).start()

    for k in range(max(nz + 2, near + 1)):
        if 1 <= k < nz + 2:
            gather_slot(0, k, 0)
        if k < near:
            a_at(k, a_near)
        if 1 <= k < near + 1:
            a_at(k - 1, a_far)
        if k == near - 1:
            for w in range(1, nw):
                gather_start(w)

    @pl.when(jnp.logical_not(primary))
    def _():
        for j in range(p.P):
            a_wait(j)

    swap.wait_recv()
    pre2[...] = jnp.where(primary, pre[...], pre2[...])
    row = here.um * p.Q + here.uq
    preu[...] = jnp.broadcast_to(pre2[pl.ds(row, 1), :], preu.shape)

    gather_wait(0)
    local[0].wait()
    cols = []
    for h in range(p.pairs):
        for k in range(3):
            start = pl.multiple_of(k * p.D + here.group * p.W + h * PAIR, PAIR)
            src = wqf.at[:, pl.ds(start, PAIR)]
            cols.append(pltpu.make_async_copy(src, wcol.at[h, :, pl.ds(k * PAIR, PAIR)], col_sem.at[h, k]))
            cols[-1].start()
    for copy in cols:
        copy.wait()
    own = pl.ds(pl.multiple_of(here.group * p.W, PAIR), p.W)
    q_bias = parf[0:1, own].astype(F32)
    v_bias = parf[1:2, own].astype(F32)

    def project(i, carry):
        rows = pl.ds(pl.multiple_of(i * BQ, BQ), BQ)
        part = a_all[rows, :]
        for h in range(p.pairs):
            lanes = slice(h * PAIR, (h + 1) * PAIR)
            got = dot(part, wcol[h])
            q_out[rows, lanes] = (got[:, :PAIR] + q_bias[:, lanes]).astype(BF16)
            k_out[rows, lanes] = got[:, PAIR : 2 * PAIR].astype(BF16)
            v_out[rows, lanes] = (got[:, 2 * PAIR :] + v_bias[:, lanes]).astype(BF16)
        return carry

    lax.fori_loop(0, p.nq, project, 0)

    prefix = preu[0:1, 0:1]
    slots = nz + 1 + LAG
    per = -(-slots // p.nq)

    def o_copy(i):
        rows = pl.ds(pl.multiple_of(i * BQ, BQ), BQ)
        home = here.uq * p.P + i // p.pieces
        piece = lax.rem(i, p.pieces)
        there = pl.ds(pl.multiple_of(piece * BQ, BQ), BQ)
        src = o_out.at[rows, :]
        dst = oh.at[here.um, there, own]
        away = jnp.logical_or(home != s, here.uc != c)
        recv = o_rs.at[here.um, here.group, piece]
        return away, lambda: remote(src, dst, o_ss.at[i], recv, home, here.chip + here.uc), (src, dst, recv)

    def attend(i, carry):
        rows = pl.ds(pl.multiple_of(i * BQ, BQ), BQ)
        row_pos = (lax.broadcasted_iota(jnp.int32, (BQ, 1), 0) + i * BQ + 1).astype(F32)
        bound = jnp.maximum(row_pos, prefix)
        key_pos = lax.broadcasted_iota(jnp.int32, (1, LEN), 1).astype(F32)
        seen = key_pos < bound

        def pair_step(h, inner):
            lanes = pl.ds(pl.multiple_of(h * PAIR, PAIR), PAIR)
            qp, kp, vp = q_out[rows, lanes], k_out[:, lanes], v_out[:, lanes]
            halves = []
            for e in (0, 1):
                logits = dot(jnp.where(head_lanes(BQ, e), qp, jnp.zeros_like(qp)), kp, 1, 1)
                logits = jnp.where(seen, logits, MASKED)
                top = jnp.max(logits, axis=1, keepdims=True)
                powers = jnp.exp2((logits - top) * SCALE2)
                total = jnp.sum(powers, axis=1, keepdims=True)
                halves.append(dot(powers.astype(BF16), vp) * (1.0 / total))
                level = top * SCALE2 + jnp.log2(total)
                turned = jnp.broadcast_to(level, (BQ, 128)).T
                lse_out[2 * h + e, :, pl.ds(pl.multiple_of(i * BQ, BQ), BQ)] = turned[0:8]
            o_out[rows, lanes] = jnp.where(head_lanes(BQ, 0), halves[0], halves[1]).astype(BF16)
            return inner

        lax.fori_loop(0, p.pairs, pair_step, 0)
        launch(*o_copy(i))

        for extra in range(per):
            for w in range(1, nw):
                gather_slot(w, i * per + extra + 1, LAG)

        return carry

    lax.fori_loop(0, p.nq, attend, 0)

    for m in range(p.M):
        for g in range(p.groups):
            for piece in range(p.pieces):
                src = o_out.at[pl.ds(0, BQ), :]
                dst = oh.at[m, pl.ds(piece * BQ, BQ), pl.ds(g * p.W, p.W)]
                pltpu.make_async_copy(src, dst, o_rs.at[m, g, piece]).wait()

    def o_sent(i, carry):
        sent(*o_copy(i))
        return carry

    lax.fori_loop(0, p.nq, o_sent, 0)
    for copy in small:
        copy.wait_send()
    swap.wait_send()
    for copy in local[1:]:
        copy.wait()
    for m in range(p.M):
        to, far = first_hop(m)

        @pl.when(to != s)
        def _():
            far().wait_send()

    @pl.when(primary)
    def _():
        for jj in range(near):
            for k in range(p.cpu):
                a_forward(jj * p.cpu + here.lane, k).wait_send()
            for k in range(1, p.cpu):
                a_forward(jj * p.cpu + lax.rem(here.lane + k, p.cpu), 0).wait_send()

    for w in range(nw):
        if w:
            gather_wait(w)
        gather_drain(w)


def fore(plan, x, par, pre, weights):
    p = plan
    nz = p.S // 2
    nw = len(weights)
    any_space = pl.BlockSpec(memory_space=pl.ANY)
    vmem = pl.BlockSpec(memory_space=pltpu.VMEM)
    shape = jax.ShapeDtypeStruct
    out_shape = (
        [shape((w.shape[0] * p.S, w.shape[1]), BF16) for w in weights]
        + [shape((par.shape[0], p.D), BF16), shape((p.M, p.T, p.D), BF16)]
        + [shape((LEN, p.W), BF16)] * 4
        + [shape((2 * p.pairs, 8, LEN), F32), shape((8, 128), F32), shape((p.M, p.T, p.D), BF16)]
        + [shape((LEN, p.D), BF16), shape((p.pairs, p.D, 3 * PAIR), BF16)]
    )
    dma = pltpu.SemaphoreType.DMA
    return pl.pallas_call(
        functools.partial(fore_kernel, p),
        out_shape=out_shape,
        in_specs=[vmem] * (3 + nw),
        out_specs=[any_space] * nw + [vmem] * 11,
        scratch_shapes=[
            pltpu.VMEM((p.S,) + par.shape, BF16),
            pltpu.VMEM((8, 128), F32),
            dma((p.S,)), dma((p.S,)), dma((2,)), dma((nw,)),
            dma((p.M,)), dma((p.P,)), dma((p.P, p.cpu)),
            dma((nw, 2, nz)), dma((nw, 2, nz)), dma((nw, nz)), dma((nw, nz)),
            dma((nw, 2, nz)), dma((nw, 2, nz)), dma((nw, 4, nz)), dma((nw, 4, nz)),
            dma((p.nq,)), dma((p.M, p.groups, p.pieces)), dma((p.pairs, 3)),
        ],
        compiler_params=pltpu.CompilerParams(
            collective_id=0, has_side_effects=True, vmem_limit_bytes=VMEM_LIMIT
        ),
        name="fore",
    )(x, par, pre, *weights)


class GridSum:
    def __init__(self, here, grads, outs, refs):
        self.here, self.grads, self.outs = here, grads, outs
        self.nw = nw = len(grads)
        self.nz = here.rows
        self.planes = here.p.R // CORES
        self.own, self.acc, self.one, self.two, self.far = (refs[k * nw : (k + 1) * nw] for k in range(5))
        (self.ld, self.m_s, self.m_r, self.a_s, self.a_r, self.b_s, self.b_r, self.z_s, self.z_r) = refs[5 * nw : 5 * nw + 9]
        (self.x_s, self.x_r, self.t_s, self.t_r, self.f_s, self.f_r) = refs[5 * nw + 9 :]
        self.side_first = SIDE_FIRST

    @staticmethod
    def scratch(plan, shapes):
        nw = len(shapes)
        planes = plan.R // CORES
        nz = plan.S // 2
        dma = pltpu.SemaphoreType.DMA
        return (
            [pltpu.VMEM((2,) + sh, BF16) for sh in shapes]
            + [pltpu.VMEM((plan.S,) + sh, BF16) for sh in shapes]
            + [
                pltpu.VMEM((plan.S, sh[0], sh[1] // 2) if sf else (nz,) + sh, BF16)
                for sh, sf in zip(shapes, SIDE_FIRST)
            ]
            + [pltpu.VMEM((nz, sh[0], sh[1] // 2), BF16) for sh in shapes]
            + [pltpu.VMEM((max(nz, planes // 2), sh[0], sh[1] // 2), BF16) for sh in shapes]
            + [dma((nw,))]
            + [dma((nw, nz))] * 8
            + [dma((nw, planes))] * 2
            + [dma((nw,))] * 2
            + [dma((nw, 2))] * 2
        )

    @staticmethod
    def count(nw):
        return 5 * nw + 15

    def zr(self, k):
        return lax.rem(self.here.row + 1 + k, self.nz)

    def half(self, w, side):
        n = self.acc[w].shape[2] // 2
        return pl.ds(pl.multiple_of(side * n, n), n)

    def load(self, w, k):
        src = self.grads[w].at[pl.ds(2 * self.zr(k), 2), self.here.c]
        return pltpu.make_async_copy(src, self.own[w], self.ld.at[w])

    def swap(self, w, k):
        here = self.here
        pair = pl.ds(2 * self.zr(k), 2)
        return remote(
            self.grads[w].at[pair, 1 - here.c], self.acc[w].at[pair], self.m_s.at[w, k], self.m_r.at[w, k], here.s, here.mate
        )

    def first(self, w, k):
        here, zr = self.here, self.zr(k)
        if self.side_first[w]:
            pair = pl.ds(2 * zr, 2)
            src = self.acc[w].at[pair, :, self.half(w, 1 - here.side)]
            return remote(src, self.one[w].at[pair], self.a_s.at[w, k], self.a_r.at[w, k], here.s, here.twin)
        src = self.acc[w].at[2 * zr + 1 - here.col]
        return remote(src, self.one[w].at[zr], self.a_s.at[w, k], self.a_r.at[w, k], here.beside, here.r)

    def second(self, w, k):
        here, zr = self.here, self.zr(k)
        if self.side_first[w]:
            src = self.acc[w].at[2 * zr + 1 - here.col, :, self.half(w, here.side)]
            to = (here.beside, here.r)
        else:
            src = self.acc[w].at[2 * zr + here.col, :, self.half(w, 1 - here.side)]
            to = (here.s, here.twin)
        return remote(src, self.two[w].at[zr], self.b_s.at[w, k], self.b_r.at[w, k], *to)

    def final(self, w, k):
        here, zr = self.here, self.zr(k)
        src = self.acc[w].at[2 * zr + here.col, :, self.half(w, here.side)]
        return remote(
            src, self.far[w].at[here.row], self.z_s.at[w, k], self.z_r.at[w, here.row], 2 * zr + here.col, here.r
        )

    def begin(self):
        for k in range(self.nz):
            for w in range(self.nw):
                self.swap(w, k).start()
                if k == 0:
                    self.load(w, 0).start()

    def event_one(self, w, k):
        zr = self.zr(k)
        pair = pl.ds(2 * zr, 2)
        self.load(w, k).wait()
        self.swap(w, k).wait_recv()
        self.acc[w][pair] = (self.acc[w][pair].astype(F32) + self.own[w][...].astype(F32)).astype(BF16)
        self.first(w, k).start()

        @pl.when(k < self.nz - 1)
        def _():
            self.load(w, jnp.minimum(k + 1, self.nz - 1)).start()

    def event_two(self, w, k):
        here, zr = self.here, self.zr(k)
        self.first(w, k).wait_recv()
        acc = self.acc[w]
        if self.side_first[w]:
            pair = pl.ds(2 * zr, 2)
            lanes = self.half(w, here.side)
            acc[pair, :, lanes] = (acc[pair, :, lanes].astype(F32) + self.one[w][pair].astype(F32)).astype(BF16)
        else:
            at = 2 * zr + here.col
            acc[at] = (acc[at].astype(F32) + self.one[w][zr].astype(F32)).astype(BF16)
        self.second(w, k).start()

    def event_three(self, w, k):
        here, zr = self.here, self.zr(k)
        self.second(w, k).wait_recv()
        at, lanes = 2 * zr + here.col, self.half(w, here.side)
        self.acc[w][at, :, lanes] = (self.acc[w][at, :, lanes].astype(F32) + self.two[w][zr].astype(F32)).astype(BF16)

        @pl.when(k < self.nz - 1)
        def _():
            self.final(w, k).start()

    def events(self):
        return self.nw * self.nz + 2 * SUM_LAG

    def event(self, n):
        for stage, body in enumerate((self.event_one, self.event_two, self.event_three)):
            e = n - stage * SUM_LAG
            for w in range(self.nw):
                ok = jnp.logical_and(e >= 0, e < self.nw * self.nz)

                @pl.when(jnp.logical_and(ok, lax.rem(e, self.nw) == w))
                def _():
                    body(w, jnp.maximum(e, 0) // self.nw)

    def over(self, w, k):
        here = self.here
        pairs = self.planes // 2
        to = 2 * lax.rem(here.plane // 2 + k, pairs) + here.side
        src = self.two[w].at[0]
        return remote(
            src, self.one_slot(w, here.plane // 2), self.x_s.at[w, k], self.x_r.at[w, here.plane // 2],
            here.s, to * CORES + here.c,
        )

    def one_slot(self, w, k):
        return self.acc[w].at[k, :, self.half(w, self.here.side)]

    def to_twin(self, w, side):
        part = self.outs[w].at[self.here.c, :, self.half(w, side)]
        return remote(part, part, self.t_s.at[w], self.t_r.at[w], self.here.s, self.here.twin)

    def to_mate(self, w, core, via):
        side = self.here.side if via == 0 else 1 - self.here.side
        part = self.outs[w].at[core, :, self.half(w, side)]
        return remote(part, part, self.f_s.at[w, via], self.f_r.at[w, via], self.here.s, self.here.mate)

    def finish(self):
        here = self.here
        for w in range(self.nw):
            self.far[w][here.row] = self.acc[w][here.s, :, self.half(w, here.side)]
            for k in range(self.nz - 1):
                off = lax.rem(here.row + 1 + k, self.nz)
                part = self.far[w].at[off]
                remote(part, part, self.z_s.at[w, k], self.z_r.at[w, off], here.s, here.r).wait_recv()
            total = self.far[w][0].astype(F32)
            for k in range(1, self.nz):
                total = total + self.far[w][k].astype(F32)
            self.outs[w][here.c, :, self.half(w, here.side)] = total.astype(BF16)
            self.to_twin(w, here.side).start()
            self.to_mate(w, here.c, 0).start()

    def twin_to_mate(self):
        for w in range(self.nw):
            self.to_twin(w, 1 - self.here.side).wait_recv()
            self.to_mate(w, self.here.c, 1).start()

    def drain(self):
        for w in range(self.nw):
            for via in (0, 1):
                self.to_mate(w, 1 - self.here.c, via).wait_recv()
                self.to_mate(w, self.here.c, via).wait_send()
            self.to_twin(w, self.here.side).wait_send()
            for k in range(self.nz):
                self.swap(w, k).wait_send()
                self.first(w, k).wait_send()
                self.second(w, k).wait_send()
                if k < self.nz - 1:
                    self.final(w, k).wait_send()


def sum_peers(here):
    p = here.p
    planes = p.R // CORES
    far = [(here.s, lax.rem(here.plane + k, planes) * CORES + j) for k in range(1, planes) for j in range(CORES)]
    twin_chip = here.twin - here.c
    return plane_peers(here) + far + [(here.beside, twin_chip + j) for j in range(CORES)]


def split_rows(p, grad):
    rows, cols = grad.shape
    return grad.reshape(p.S, CORES, rows // (p.S * CORES), cols)


def whole_shard(halves):
    return halves.reshape(CORES * halves.shape[1], halves.shape[2]).astype(F32)


def back_kernel(plan, nw, *refs):
    p = plan
    here = Place(p)
    s, c = here.s, here.c
    nz, near, width = here.rows, p.near, p.width
    (q, k, v, o, lse, preu, do_home, a_all, wcol, x, stream, par, small) = refs[:13]
    grads = refs[13 : 13 + nw]
    rest = refs[13 + nw :]
    input_grad, gq, small_out = rest[:3]
    outs = rest[3 : 3 + nw]
    rest = rest[3 + nw :]
    (do_all, low, dk_acc, dv_acc, k_turn, da_own, da_out, da_in, da_side) = rest[:9]
    x_buf, stream_buf, buf_sem, a_buf, a_sem = rest[-5:]
    rest = rest[:-5]
    da_home = input_grad
    (dw_out, dw_own, dw_in, dw_far, dw_end, small_acc, small_in, small_all) = rest[9:17]
    (do_ss, do_rs, dm_s, dm_r, dy_s, dy_r, dh_s, dh_r, wt_s, wt_r, wz_s, wz_r, wx_s, wx_r, wd_s, wd_r) = rest[17:33]
    (ss_s, ss_r, sa_s, sa_r) = rest[33:37]
    sums = GridSum(here, grads, outs, rest[37:])
    per = -(-sums.events() // (p.pairs * p.nq))
    greet(sum_peers(here))
    rows_here = pl.ds(pl.multiple_of(lax.rem(s, p.P) * p.T, p.T), p.T)

    def do_copy(m, g):
        core, lane = g // p.cpu, g % p.cpu
        to = here.unit_of(c, m, s) * p.cpu + lane
        src = do_home.at[m, :, pl.ds(g * p.W, p.W)]
        dst = do_all.at[rows_here, :]
        away = jnp.logical_or(to != s, c != core)
        recv = do_rs.at[lax.rem(s, p.P)]
        return away, lambda: remote(src, dst, do_ss.at[m, g], recv, to, here.chip + core), (src, dst, recv)

    for m in range(p.M):
        for g in range(p.groups):
            launch(*do_copy(m, g))
    sums.begin()
    small_acc[...] = small[...]
    prefix = preu[0:1, 0:1]

    def block_rows(i):
        return pl.ds(pl.multiple_of(i * BQ, BQ), BQ)

    def a_load(b):
        slot = lax.rem(b, 2)
        return pltpu.make_async_copy(
            a_all.at[:, pl.ds(pl.multiple_of(b * BQ, BQ), BQ)], a_buf.at[slot], a_sem.at[slot]
        )

    def weight_part(h, dst):
        def some(b, carry):
            slot = lax.rem(b, 2)

            @pl.when(b < p.D // BQ - 1)
            def _():
                a_load(b + 1).start()

            a_load(b).wait()
            dst[pl.ds(pl.multiple_of(b * BQ, BQ), BQ), :] = dot(a_buf[slot], low[h], 0, 0).astype(BF16)
            return carry

        lax.fori_loop(0, p.D // BQ, some, 0)

    def bias_part(h):
        folds = PAIR // width
        for row, lanes in ((0, slice(0, PAIR)), (1, slice(2 * PAIR, 3 * PAIR))):
            total = jnp.sum(low[h, :, lanes].astype(F32), axis=0, keepdims=True)
            for n in range(folds):
                at = (here.group * p.pairs + h) * folds + n
                small_acc[at, row : row + 1, 0:width] = total[:, n * width : (n + 1) * width]

    def to_twin_dw():
        return remote(dw_out, dw_in, wt_s.at[0], wt_r.at[0], s, here.twin)

    def pair_step(turn, carry):
        h = lax.rem(turn + 1 + here.side, 2)
        lanes = pl.ds(pl.multiple_of(h * PAIR, PAIR), PAIR)
        k_turn[...] = k[:, lanes].astype(F32).T.astype(BF16)
        dk_acc[...] = jnp.zeros_like(dk_acc)
        dv_acc[...] = jnp.zeros_like(dv_acc)

        def query_step(i, inner):
            rows = block_rows(i)

            @pl.when(jnp.logical_and(turn == 0, lax.rem(i, p.pieces) == 0))
            def _():
                j = i // p.pieces
                part = do_all.at[pl.ds(pl.multiple_of(j * p.T, p.T), p.T), :]
                pltpu.make_async_copy(part, part, do_rs.at[j]).wait()

            qp, dop, op = q[rows, lanes], do_all[rows, lanes], o[rows, lanes]
            turned = (dop.astype(F32) * op.astype(F32)).T
            pos = (lax.broadcasted_iota(jnp.int32, (1, BQ), 1) + i * BQ + 1).astype(F32)
            bound = jnp.maximum(pos, prefix)
            dq_t = []
            for e in (0, 1):
                lit = head_lanes(BQ, e)
                qe = jnp.where(lit, qp, jnp.zeros_like(qp))
                de = jnp.where(lit, dop, jnp.zeros_like(dop))
                level = lse[2 * h + e, 0:1, rows]
                inner_sum = jnp.sum(turned[e * HEAD : (e + 1) * HEAD], axis=0, keepdims=True)
                total = jnp.zeros((HEAD, BQ), F32)
                for start in range(0, LEN, KEYS):
                    keys = slice(start, start + KEYS)
                    key_pos = (lax.broadcasted_iota(jnp.int32, (KEYS, 1), 0) + start).astype(F32)
                    logits = dot(k[keys, lanes], qe, 1, 1)
                    probs = jnp.where(key_pos < bound, jnp.exp2(logits * SCALE2 - level), 0.0)
                    slope = dot(v[keys, lanes], de, 1, 1)
                    dlog = (probs * (slope - inner_sum)).astype(BF16)
                    dv_acc[keys, :] += dot(probs.astype(BF16), de)
                    dk_acc[keys, :] += dot(dlog, qe)
                    total = total + dot(k_turn[e * HEAD : (e + 1) * HEAD, keys], dlog)
                dq_t.append(total)
            low[h, rows, 0:PAIR] = (jnp.concatenate(dq_t, axis=0).T * SCALE).astype(BF16)
            for extra in range(per):
                sums.event((turn * p.nq + i) * per + extra)
            return inner

        lax.fori_loop(0, p.nq, query_step, 0)
        low[h, :, PAIR : 2 * PAIR] = (dk_acc[...] * SCALE).astype(BF16)
        low[h, :, 2 * PAIR :] = dv_acc[...].astype(BF16)
        bias_part(h)

        a_load(0).start()

        @pl.when(turn == 0)
        def _():
            weight_part(h, dw_out)
            to_twin_dw().start()

        return carry

    lax.fori_loop(0, p.pairs, pair_step, 0)

    half = p.D // CORES

    def block_of(n):
        lane = lax.rem(here.lane + 1 + n // (near * p.pieces), p.cpu)
        m = lax.rem(n, near * p.pieces)
        return ((m // p.pieces) * p.cpu + lane) * p.pieces + lax.rem(m, p.pieces)

    def da_half(rows, core):
        at = pl.ds(pl.multiple_of(core * half, half), half)
        total = dot(low[0, rows, :], wcol[0, at, :], 1, 1)
        for h in range(1, p.pairs):
            total = total + dot(low[h, rows, :], wcol[h, at, :], 1, 1)
        return total

    def da_mate(n, i):
        rows = block_rows(i)
        return remote(da_out.at[rows, :], da_in.at[rows, :], dm_s.at[n], dm_r.at[i], s, here.mate)

    def da_first(n, carry):
        i = block_of(n)
        rows = block_rows(i)
        da_out[rows, :] = da_half(rows, 1 - c).astype(BF16)
        da_mate(n, i).start()
        da_own[rows, :] = da_half(rows, c).astype(BF16)
        return carry

    lax.fori_loop(0, p.nq, da_first, 0)

    own_pair = here.side
    weight_part(own_pair, dw_own)
    to_twin_dw().wait_recv()
    dw_own[...] = (dw_own[...].astype(F32) + dw_in[...].astype(F32)).astype(BF16)
    span = 2 * width

    def dw_rows(zr):
        return pl.ds(pl.multiple_of(zr * span, span), span)

    def dw_send(n):
        zr = lax.rem(here.row + 1 + n, nz)
        return remote(
            dw_own.at[dw_rows(zr), :], dw_far.at[here.row], wz_s.at[n], wz_r.at[here.row], 2 * zr + here.col, here.r
        )

    for n in range(nz - 1):
        dw_send(n).start()

    far_blocks = (p.cpu - 1) * near * p.pieces

    def side_rows(i):
        return block_rows((i // p.pieces // p.cpu) * p.pieces + lax.rem(i, p.pieces))

    def da_over(n, i):
        return remote(da_own.at[block_rows(i), :], da_side.at[side_rows(i), :], dy_s.at[n], dy_r.at[i], here.beside, here.r)

    def da_back(n, i):
        rows = block_rows(i)
        home = here.uq * p.P + i // p.pieces
        piece = lax.rem(i, p.pieces)
        dst = da_home.at[here.um, block_rows(piece), pl.ds(pl.multiple_of(c * half, half), half)]
        src = da_own.at[rows, :]
        recv = dh_r.at[here.um, c, piece]
        away = jnp.logical_or(home != s, here.uc != c)
        return away, lambda: remote(src, dst, dh_s.at[n], recv, home, here.chip + here.uc), (src, dst, recv)

    def da_second(n, carry):
        i = block_of(n)
        rows = block_rows(i)
        da_mate(n, i).wait_recv()
        pair = da_own[rows, :].astype(F32) + da_in[rows, :].astype(F32)

        @pl.when(n < far_blocks)
        def _():
            da_own[rows, :] = pair.astype(BF16)
            da_over(n, i).start()

        @pl.when(n >= far_blocks)
        def _():
            da_over(n, i).wait_recv()
            da_own[rows, :] = (pair + da_side[side_rows(i), :].astype(F32)).astype(BF16)
            launch(*da_back(n, i))

        return carry

    lax.fori_loop(0, p.nq, da_second, 0)
    sums.finish()

    dw_far[here.row] = dw_own[dw_rows(here.row), :]
    for n in range(nz - 1):
        off = lax.rem(here.row + 1 + n, nz)
        remote(dw_far.at[off], dw_far.at[off], wz_s.at[n], wz_r.at[off], s, here.r).wait_recv()
    total = dw_far[0].astype(F32)
    for n in range(1, nz):
        total = total + dw_far[n].astype(F32)
    dw_end[...] = total.astype(BF16)
    slot = here.group * p.pairs + here.side
    twin_chip = here.twin - c

    def dw_give(n):
        fy, fx, fc = n // 4, n // 2 % 2, n % 2
        col = here.col if fy == 0 else 1 - here.col
        core = c if fc == 0 else 1 - c
        src = dw_end.at[pl.ds(pl.multiple_of(col * width, width), width), :]
        dst = gq.at[slot]
        to = (2 * here.row + col, (here.chip if fx == 0 else twin_chip) + core)
        return src, dst, to

    for n in range(1, 8):
        src, dst, to = dw_give(n)
        remote(src, dst, wd_s.at[n], wd_r.at[slot], *to).start()
    gq[slot] = dw_end[pl.ds(pl.multiple_of(here.col * width, width), width), :]

    def token_loads(m, piece):
        at = pl.ds(piece * BQ, BQ)
        return (
            pltpu.make_async_copy(x.at[m, at, :], x_buf, buf_sem.at[0]),
            pltpu.make_async_copy(stream.at[m, at, :], stream_buf, buf_sem.at[1]),
        )

    for copy in token_loads(0, 0):
        copy.start()
    gain = par[4:5, :].astype(F32)
    gain_sum = jnp.zeros((1, p.D), F32)
    shift_sum = jnp.zeros((1, p.D), F32)
    for m in range(p.M):
        for piece in range(p.pieces):
            at = slice(piece * BQ, (piece + 1) * BQ)
            for core in range(CORES):
                dst = da_home.at[m, pl.ds(piece * BQ, BQ), pl.ds(core * half, half)]
                pltpu.make_async_copy(dst, dst, dh_r.at[m, core, piece]).wait()
            for copy in token_loads(m, piece):
                copy.wait()
            values = x_buf[...].astype(F32)
            dy = da_home[m, at, :].astype(F32)
            centre = values - jnp.mean(values, axis=-1, keepdims=True)
            spread = jnp.mean(centre * centre, axis=-1, keepdims=True)
            scale = lax.rsqrt(spread + EPS)
            wn = centre * scale
            e = dy * gain
            dw = scale * (e - jnp.mean(e, axis=-1, keepdims=True) - wn * jnp.mean(e * wn, axis=-1, keepdims=True))
            input_grad[m, at, :] = (stream_buf[...] + dw).astype(BF16)
            if m * p.pieces + piece + 1 < p.M * p.pieces:
                follow = m * p.pieces + piece + 1
                for copy in token_loads(follow // p.pieces, follow % p.pieces):
                    copy.start()
            gain_sum = gain_sum + jnp.sum(dy * wn, axis=0, keepdims=True)
            shift_sum = shift_sum + jnp.sum(dy, axis=0, keepdims=True)
    for n in range(p.S):
        lanes = slice(n * width, (n + 1) * width)
        small_acc[n, 4:5, 0:width] = gain_sum[:, lanes]
        small_acc[n, 8:9, 0:width] = shift_sum[:, lanes]

    def tiny(n):
        to = lax.rem(s + n, p.S)
        return remote(small_acc.at[to], small_in.at[n], ss_s.at[n], ss_r.at[n], to, here.r)

    for n in range(1, p.S):
        tiny(n).start()
    sums.twin_to_mate()
    total = small_acc[s]
    for n in range(1, p.S):
        tiny(n).wait_recv()
        total = total + small_in[n]
    small_all[here.r] = total

    def every(n):
        to = lax.rem(here.r + n, p.R)
        return remote(small_all.at[here.r], small_all.at[here.r], sa_s.at[n], sa_r.at[here.r], s, to)

    for n in range(1, p.R):
        every(n).start()
    for n in range(1, p.R):
        off = lax.rem(here.r + n, p.R)
        remote(small_all.at[0], small_all.at[off], sa_s.at[n], sa_r.at[off], s, here.r).wait_recv()
    total = small_all[0]
    for n in range(1, p.R):
        total = total + small_all[n]
    small_out[...] = total

    for m in range(p.M):
        for g in range(p.groups):
            sent(*do_copy(m, g))

    def da_sent(n, carry):
        i = block_of(n)
        da_mate(n, i).wait_send()

        @pl.when(n < far_blocks)
        def _():
            da_over(n, i).wait_send()

        @pl.when(n >= far_blocks)
        def _():
            sent(*da_back(n, i))

        return carry

    lax.fori_loop(0, p.nq, da_sent, 0)
    to_twin_dw().wait_send()
    for n in range(nz - 1):
        dw_send(n).wait_send()
    for n in range(1, 8):
        src, dst, to = dw_give(n)
        remote(src, dst, wd_s.at[n], wd_r.at[slot], *to).wait_send()
    for n in range(p.groups * p.pairs):

        @pl.when(n != slot)
        def _():
            remote(gq.at[n], gq.at[n], wd_s.at[0], wd_r.at[n], s, here.r).wait_recv()

    for n in range(1, p.S):
        tiny(n).wait_send()
    for n in range(1, p.R):
        every(n).wait_send()
    sums.drain()


def back(plan, units, small, grads):
    p = plan
    nw = len(grads)
    nz = p.S // 2
    planes = p.R // CORES
    split = [split_rows(p, grad) for grad in grads]
    shapes = [h.shape[2:] for h in split]
    any_space = pl.BlockSpec(memory_space=pl.ANY)
    vmem = pl.BlockSpec(memory_space=pltpu.VMEM)
    dma = pltpu.SemaphoreType.DMA
    shape = jax.ShapeDtypeStruct
    half = p.D // CORES
    outs = pl.pallas_call(
        functools.partial(back_kernel, p, nw),
        out_shape=[
            shape((p.M, p.T, p.D), BF16),
            shape((p.groups * p.pairs, p.width, 3 * PAIR), BF16),
            shape(small.shape[1:], F32),
        ]
        + [shape((CORES,) + sh, BF16) for sh in shapes],
        in_specs=[vmem] * 6 + [any_space] * 2 + [vmem] + [any_space] * 2 + [vmem] * 2 + [any_space] * nw,
        out_specs=[vmem] * (3 + nw),
        scratch_shapes=[
            pltpu.VMEM((LEN, p.W), BF16),
            pltpu.VMEM((p.pairs, LEN, 3 * PAIR), BF16),
            pltpu.VMEM((LEN, PAIR), F32),
            pltpu.VMEM((LEN, PAIR), F32),
            pltpu.VMEM((PAIR, LEN), BF16),
            pltpu.VMEM((LEN, half), BF16),
            pltpu.VMEM((LEN, half), BF16),
            pltpu.VMEM((LEN, half), BF16),
            pltpu.VMEM((p.near * p.T, half), BF16),
            pltpu.VMEM((p.D, 3 * PAIR), BF16),
            pltpu.VMEM((p.D, 3 * PAIR), BF16),
            pltpu.VMEM((p.D, 3 * PAIR), BF16),
            pltpu.VMEM((nz, 2 * p.width, 3 * PAIR), BF16),
            pltpu.VMEM((2 * p.width, 3 * PAIR), BF16),
            pltpu.VMEM(small.shape, F32),
            pltpu.VMEM(small.shape, F32),
            pltpu.VMEM((p.R,) + small.shape[1:], F32),
            dma((p.M, p.groups)), dma((p.P,)),
            dma((p.nq,)), dma((p.nq,)), dma((p.nq,)), dma((p.nq,)),
            dma((p.nq,)), dma((p.M, CORES, p.pieces)),
            dma((1,)), dma((1,)), dma((nz,)), dma((nz,)), dma((planes,)), dma((planes,)), dma((8,)), dma((8,)),
            dma((p.S,)), dma((p.S,)), dma((p.R,)), dma((p.R,)),
        ]
        + GridSum.scratch(p, shapes)
        + [pltpu.VMEM((BQ, p.D), BF16), pltpu.VMEM((BQ, p.D), F32), dma((2,))]
        + [pltpu.VMEM((2, LEN, BQ), BF16), dma((2,))],
        compiler_params=pltpu.CompilerParams(
            collective_id=1, has_side_effects=True, vmem_limit_bytes=VMEM_LIMIT
        ),
        name="back",
    )(*units, small, *split)
    gq = outs[1].reshape(p.groups, p.pairs, p.width, 3, PAIR).transpose(2, 3, 0, 1, 4).reshape(p.width, 3 * p.D)
    return outs[0], gq.astype(F32), outs[2], [whole_shard(part) for part in outs[3:]]


def per_device(
    sizes,
    inputs,
    prefix,
    qkv_weight,
    qv_bias,
    out_weight,
    branch_bias,
    up_weight,
    up_bias,
    down_weight,
    norm_gain,
    norm_bias,
    cotangent,
):
    p = Plan(sizes, (inputs.shape[0], 1, inputs.shape[2], inputs.shape[3]))
    tokens_all = p.M * p.T
    x = inputs[:, 0]
    width = p.D // p.S
    spare = max(128 - width, 0)
    par = jnp.concatenate([qv_bias, branch_bias, norm_gain, norm_bias, up_bias.reshape(-1, width)], axis=0)
    par = jnp.pad(par, ((0, 0), (0, spare)))
    pre = jnp.broadcast_to(prefix[:, 0].reshape(-1, 1).astype(F32), (p.M * p.Q, 128))
    pre = jnp.pad(pre, ((0, 8 - p.M * p.Q), (0, 0)))
    (_, wo, wu, wd, parf, _, q, k, v, o, lse, preu, o_home, a_unit, w_unit) = fore(
        p, x, par, pre, (qkv_weight, out_weight, up_weight, down_weight)
    )
    par32 = parf.astype(F32)
    bias_branch = par32[2:4]
    gains, shifts = par32[4:8], par32[8:12]
    bias_up = par32[12:].reshape(-1, p.S, width).transpose(1, 0, 2).reshape(-1)

    tokens = x.reshape(tokens_all, p.D).astype(F32)
    upstream = cotangent[:, 0].reshape(tokens_all, p.D).astype(F32)
    mixed_low = o_home.reshape(tokens_all, p.D)
    branch = dot(mixed_low, wo) + bias_branch[0]
    side, pull_side = jax.vjp(normed, branch, gains[1:2], shifts[1:2])
    stream = tokens + side
    normal_mid, pull_mid = jax.vjp(normed, stream, gains[2:3], shifts[2:3])
    middle_low = normal_mid.astype(BF16)
    upper = dot(middle_low, wu) + bias_up
    below = 0.5 * (1.0 + lax.erf(upper * math.sqrt(0.5)))
    slope = below + upper * jnp.exp(-0.5 * upper * upper) * (1.0 / math.sqrt(2.0 * math.pi))
    active_low, slope = lax.optimization_barrier(((upper * below).astype(BF16), slope))
    lower = dot(active_low, wd) + bias_branch[1]
    closing, pull_close = jax.vjp(normed, lower, gains[3:4], shifts[3:4])
    output = (stream + closing).astype(BF16)
    grad_lower, gain_three, shift_three = pull_close(upstream)
    lower_low = grad_lower.astype(BF16)
    grad_active = dot(lower_low, wd, 1, 1)
    upper_low = (grad_active * slope).astype(BF16)
    grad_middle = dot(upper_low, wu, 1, 1)
    grad_mid_in, gain_two, shift_two = pull_mid(grad_middle)
    grad_stream = grad_mid_in + upstream
    grad_branch, gain_one, shift_one = pull_side(grad_stream)
    branch_low = grad_branch.astype(BF16)
    grad_mixed = dot(branch_low, wo, 1, 1).astype(BF16)

    grads = (
        dot(active_low, lower_low, 0, 0).astype(BF16),
        dot(middle_low, upper_low, 0, 0).astype(BF16),
        dot(mixed_low, branch_low, 0, 0).astype(BF16),
    )
    def column_sum(values):
        return jnp.sum(values.astype(F32), axis=0, keepdims=True)

    du_sum = column_sum(upper_low).reshape(p.S, -1, width).transpose(1, 0, 2).reshape(-1, p.D)
    none = jnp.zeros((1, p.D), F32)
    small = jnp.concatenate(
        [
            none, none, column_sum(branch_low), column_sum(lower_low),
            none, gain_one, gain_two, gain_three,
            none, shift_one, shift_two, shift_three,
            du_sum,
        ], axis=0,
    )
    small = jnp.pad(small.reshape(-1, p.S, width).transpose(1, 0, 2), ((0, 0), (0, 0), (0, spare)))
    by_token = (p.M, p.T, p.D)
    input_grad, sum_qkv, tiny, (sum_down, sum_up, sum_out) = back(
        p,
        (
            q, k, v, o, lse, preu, grad_mixed.reshape(by_token), a_unit, w_unit,
            x, grad_stream.reshape(by_token), parf,
        ),
        small, grads,
    )
    tiny = tiny[:, :width]
    shaped = (p.M, 1, p.T, p.D)
    return (
        output.reshape(shaped),
        input_grad.reshape(shaped),
        sum_qkv,
        tiny[0:2],
        sum_out,
        tiny[2:4],
        sum_up,
        tiny[12:].reshape(-1),
        sum_down,
        tiny[4:8],
        tiny[8:12],
    )


def solution(mesh):
    sizes = {name: mesh.shape[name] for name in ("shard", "replica")}
    placed = (
        P(None, "replica", "shard", None),
        P(None, "replica", None),
        P("shard", None),
        P(None, "shard"),
        P("shard", None),
        P(None, "shard"),
        P("shard", None),
        P("shard"),
        P("shard", None),
        P(None, "shard"),
        P(None, "shard"),
        P(None, "replica", "shard", None),
    )
    return jax.shard_map(
        functools.partial(per_device, sizes),
        mesh=mesh,
        in_specs=placed,
        out_specs=(
            P(None, "replica", "shard", None),
            P(None, "replica", "shard", None),
            P("shard", None),
            P(None, "shard"),
            P("shard", None),
            P(None, "shard"),
            P("shard", None),
            P("shard"),
            P("shard", None),
            P(None, "shard"),
            P(None, "shard"),
        ),
        check_vma=False,
    )
```

time: 638 us -> 476 us (0.75)
  the two profiles are of different devices: /device:TPU:0 before, /device:TPU:25 now
where the time goes in v2:
time: 476 us; the launch traced here: 467 us
  Pallas kernels  374 us (79%)
  matrix products  62.7 us (13%)
  local copies, waits for them, and re-layouts  15.5 us (3%)
  other arithmetic  13.1 us (3%)
    pallas_call x1, Pallas kernels, back(): pl.pallas_call(functools.partial(back_kernel, p, nw), out_shape=[shape((p...  204 us
    pallas_call x1, Pallas kernels, fore(): pl.pallas_call(functools.partial(fore_kernel, p), out_shape=out_shape, in...  169 us
    dot_general x9, matrix products, dot(): lax.dot_general(a, b, (((ca,), (cb,)), ((), ())), preferred_element_type=...  62.7 us

profile of v2, /device:TPU:25, one launch (start us, length us, event | category | flops | bytes accessed | tf_op | source)
XLA Modules:
  0.0 466.5 jit_solution(13105942315771799363)
XLA Ops:
  0.6 2.6 concatenate.26.par
  3.3 0.7 convert_bitcast_fusion
  3.9 0.7 pad.7.pre
  4.6 169.4 %fore.1 = (bf16[1024,3072]{1,0:T(8,128)(2,1)}, bf16[1024,1024]{1,0:T(8,128)(2,1)}, bf16[1024,4096]{1,0:T(8,128)(2,1)}, bf16[4096,1024]{1,0:T(8,128)(2,1)}, bf16[...) custom-call(bf16[2,256,1024]{2,1,0:T(8,128)(2,1)} %bitcast.93, ...), custom_call_target="tpu_custom_call" | custom-call | tf_op jit(solution)/shard_map/fore/pallas_call | solution.py:566
  174.0 0.9 fusion.16
  175.0 0.7 slice.72
  175.7 3.4 add_reduce_fusion.1
  179.5 0.8 copy-done.2
  180.3 0.8 fusion.15
  181.6 11.5 %fusion.3 = (f32[512,4096]{1,0:T(8,128)}, bf16[512,4096]{1,0:T(8,128)(2,1)}) fusion(f32[4096]{0:T(1024)S(1)} %bitcast.126, bf16[1024,4096]{1,0:T(8,128)(2,1)S(1)} %bitcast.138, f32[512,1024]{1,0:T(8,128)S(1)} %get-tuple-element.106, f32[1024]{0:T(1024)S(1)} %bitcast.132, f32[1024]{0:T(1024)S(1)} %bitcast.128, f32[512]{0:T(512)S(1)} %fusion.9, ...), kind=kOutput, calls=%fused_computation.4 | convolution fusion | flops 4320657408 | bytes 23097344 | tf_op jit(solution)/shard_map/dot_general | solution.py:133
  193.1 6.8 %add_reduce_fusion = (f32[512]{0:T(512)S(1)}, f32[512,1024]{1,0:T(8,128)S(1)}) fusion(f32[1024]{0:T(1024)S(1)} %bitcast.112, bf16[512,4096]{1,0:T(8,128)(2,1)} %get-tuple-element.36, bf16[4096,1024]{1,0:T(8,128)(2,1)S(1)} %bitcast.140), kind=kOutput, calls=%fused_computation.37 | convolution fusion | flops 4296015360 | bytes 14686208 | tf_op jit(solution)/shard_map/dot_general | solution.py:133
  200.3 0.8 copy-done.1
  201.1 0.9 fusion.7
  202.1 2.0 fusion.14
  204.4 10.8 %convert_reduce_fusion = (f32[4096]{0:T(1024)S(1)}, bf16[512,4096]{1,0:T(8,128)(2,1)}) fusion(f32[512,4096]{1,0:T(8,128)} %get-tuple-element.44, bf16[512,1024]{1,0:T(8,128)(2,1)S(1)} %get-tuple-element.95, bf16[4096,1024]{1,0:T(8,128)(2,1)} %get-tuple-element.37), kind=kOutput, calls=%fused_computation.5 | convolution fusion | flops 4303351808 | bytes 22036480 | tf_op jit(solution)/shard_map/dot_general | solution.py:133
  215.2 8.7 %multiply_reduce_fusion = (f32[1024]{0:T(1024)S(1)}, f32[512]{0:T(512)S(1)}, f32[1024]{0:T(1024)S(1)}, f32[512,1024]{1,0:T(8,128)S(1)}) fusion(f32[512,1024]{1,0:T(8,128)S(1)} %get-tuple-element.106, f32[512]{0:T(512)S(1)} %fusion.9, f32[512]{0:T(512)S(1)} %broadcast_multiply_fusion.1, f32[1024]{0:T(1024)S(1)} %bitcast.129, ...), kind=kOutput, calls=%fused_computation.23 | convolution fusion | flops 4299159040 | bytes 16795648 | tf_op jit(solution)/shard_map/dot_general | solution.py:133
  223.9 0.7 fusion.13
  224.7 1.2 multiply_reduce_fusion.1
  225.9 0.8 fusion.12
  227.5 1.7 copy-done.10
  229.2 2.3 convolution_convert_fusion.3
  231.7 1.3 concatenate.36
  233.0 9.4 %convolution_convert_fusion.1 = bf16[4096,1024]{1,0:T(8,128)(2,1)} fusion(bf16[512,4096]{1,0:T(8,128)(2,1)} %get-tuple-element.36, bf16[512,1024]{1,0:T(8,128)(2,1)S(1)} %get-tuple-element.95), kind=kOutput, calls=%fused_computation.10 | convolution fusion | flops 4299161600 | bytes 13631488 | tf_op jit(solution)/shard_map/dot_general | solution.py:133
  242.4 7.2 %convolution_convert_fusion = bf16[1024,4096]{1,0:T(8,128)(2,1)} fusion(bf16[512,4096]{1,0:T(8,128)(2,1)S(1)} %copy-done.12, f32[512,1024]{1,0:T(8,128)S(1)} %get-tuple-element.106, f32[1024]{0:T(1024)S(1)} %bitcast.133, f32[1024]{0:T(1024)S(1)} %bitcast.131, f32[512]{0:T(512)S(1)} %fusion.9, f32[512]{0:T(512)S(1)} %broadcast_multiply_fusion.1), kind=kOutput, calls=%fused_computation.9 | convolution fusion | flops 4301783040 | bytes 14692352 | tf_op jit(solution)/shard_map/dot_general | solution.py:133
  249.6 2.6 convolution_convert_fusion.2
  252.2 204.4 %back.1 = (bf16[2,256,1024]{2,1,0:T(8,128)(2,1)}, bf16[8,128,384]{2,1,0:T(8,128)(2,1)}, f32[16,128]{1,0:T(8,128)}, bf16[2,256,1024]{2,1,0:T(8,128)(2,1)}, bf16[2...) custom-call(bf16[2048,256]{1,0:T(8,128)(2,1)} %get-tuple-element.38.refs_0_, ...), custom_call_target="tpu_custom_call" | custom-call | tf_op jit(solution)/shard_map/back/pallas_call | solution.py:1157
  456.6 1.4 copy.31
  458.2 1.6 copy.35
  460.4 0.9 bitcast_convert_fusion.2
  461.3 1.6 bitcast_convert_fusion.1
  463.5 1.6 bitcast_convert_fusion
  465.1 1.0 copy.37
  (57 shorter events, 3.9 us)
Async XLA Ops:
  175.7 5.8 %slice-start = ((s8[8388608]{0:T(1024)(128)(4,1)}), s8[4194304]{0:T(1024)(128)(4,1)S(1)}, s32[]{:S(2)}) async-start(s8[8388608]{0:T(1024)(128)(4,1)} %bitcast.137), calls=%async_computation | async-start | bytes 8388608
  179.1 1.2 copy-start.2
  179.1 2.5 slice-start.1
  181.1 12.0 %slice-start.2 = ((s8[8388608]{0:T(1024)(128)(4,1)}), s8[4194304]{0:T(1024)(128)(4,1)S(1)}, s32[]{:S(2)}) async-start(s8[8388608]{0:T(1024)(128)(4,1)} %bitcast.139), calls=%async_computation.2 | async-start | bytes 8388608
  181.6 11.5 %slice-start.3 = ((s8[8388608]{0:T(1024)(128)(4,1)}), s8[4194304]{0:T(1024)(128)(4,1)S(1)}, s32[]{:S(2)}) async-start(s8[8388608]{0:T(1024)(128)(4,1)} %bitcast.139), calls=%async_computation.3 | async-start | bytes 8388608
  199.9 1.2 copy-start.1
  225.9 1.3 copy-start
  227.2 2.0 copy-start.10
  227.5 4.0 copy-start.5
  233.0 9.4 %copy-start.12 = (bf16[512,4096]{1,0:T(8,128)(2,1)S(1)}, bf16[512,4096]{1,0:T(8,128)(2,1)}, u32[]{:S(2)}) copy-start(bf16[512,4096]{1,0:T(8,128)(2,1)} %get-tuple-element.129) | copy-start | bytes 12582916
  242.4 7.2 %copy-start.6 = (bf16[512,1024]{1,0:T(8,128)(2,1)S(1)}, bf16[512,1024]{1,0:T(8,128)(2,1)}, u32[]{:S(2)}) copy-start(bf16[512,1024]{1,0:T(8,128)(2,1)} %copy-done.5) | copy-start | bytes 3145732
  242.4 7.2 %copy-start.11 = (bf16[2,256,1024]{2,1,0:T(8,128)(2,1)S(1)}, bf16[2,256,1024]{2,1,0:T(8,128)(2,1)}, u32[]{:S(2)}) copy-start(bf16[2,256,1024]{2,1,0:T(8,128)(2,1)} %get-tuple-element.32) | copy-start | bytes 3145732
  458.2 1.6 copy-start.9
  458.2 2.2 copy-start.8
  458.2 3.1 copy-start.4
  459.8 3.6 copy-start.3
  462.9 2.2 copy-start.7

commit v3 on v2

--- a/solution.py
+++ b/solution.py
@@ -23,9 +23,12 @@
 VMEM_LIMIT = 66_000_000
 LAG = 2
 KEYS = 512
-SIDE_FIRST = (False, True, True)
-SUM_LAG = 2
-COLUMN_FIRST = (True, True, True, False)
+SIDE_FIRST = (True, False, False)
+SUM_LAG = 5
+CADENCE = 1
+COLUMN_FIRST = (True, True, False)
+START = 1
+EARLY = 1
 
 
 class Plan:
@@ -140,15 +143,15 @@
 
 def fore_kernel(
     plan, x, par, pre, wq, wo, wu, wd,
-    wqf, wof, wuf, wdf, parf, ah, q_out, k_out, v_out, o_out, lse_out, preu, oh, a_all, wcol,
+    wof, wuf, wdf, parf, ah, q_out, k_out, v_out, o_out, lse_out, preu, oh, a_all, wcol,
     parg, pre2,
     par_ss, par_rs, pre_sem, loc_sem, a_ss, a_rs, af_ss, z_ss, z_rs, wa_ss, wa_rs, wb_ss, wb_rs, wm_ss, wm_rs,
-    o_ss, o_rs, col_sem,
+    o_ss, o_rs, q_ss, q_rs, qt_ss, qt_rs, q_loc,
 ):
     p = plan
     here = Place(p)
     s, c = here.s, here.c
-    mine, full = (wq, wo, wu, wd), (wqf, wof, wuf, wdf)
+    mine, full = (wo, wu, wd), (wof, wuf, wdf)
     nw = len(mine)
     first = COLUMN_FIRST
     greet(plane_peers(here) + [(s, here.twin)])
@@ -219,13 +222,14 @@
     def can_send(d):
         return z < nz - 1 if d == 0 else z > 0
 
-    def gather_start(w):
+    def gather_rows(w):
         for d in (0, 1):
 
             @pl.when(can_send(d))
             def _():
                 z_send(w, d, 1).start()
 
+    def gather_near(w):
         if first[w]:
             to_first(w, z, origin(w, 0)).start()
         else:
@@ -333,7 +337,34 @@
 
         lax.fori_loop(0, nz, one, 0)
 
-    gather_start(0)
+    nq_rows = wq.shape[2]
+    half_rows = nq_rows // 2
+
+    def q_rows(k, side):
+        return pl.ds(pl.multiple_of(k * nq_rows + side * half_rows, half_rows), half_rows)
+
+    def q_send(k):
+        to = lax.rem(s + k, p.S)
+        group = c * p.cpu + lax.rem(to, p.cpu)
+        rows = pl.ds(pl.multiple_of(here.side * half_rows, half_rows), half_rows)
+        src = wq.at[group, :, rows, :]
+        return remote(src, wcol.at[:, q_rows(s, here.side), :], q_ss.at[k], q_rs.at[s], to, here.r)
+
+    def q_twin(k, side):
+        part = wcol.at[:, q_rows(k, side), :]
+        return remote(part, part, qt_ss.at[k], qt_rs.at[k], s, here.twin)
+
+    def q_from(k):
+        return lax.rem(s + p.S - k, p.S)
+
+    for k in range(1, p.S):
+        q_send(k).start()
+    for w in range(nw):
+        gather_near(w)
+    q_own = pltpu.make_async_copy(
+        wq.at[here.group], wcol.at[:, pl.ds(pl.multiple_of(s * nq_rows, nq_rows), nq_rows), :], q_loc.at[0]
+    )
+    q_own.start()
     local = []
     for w in range(nw):
         n = mine[w].shape[0]
@@ -411,16 +442,22 @@
             a_wait(j)
             a_forward(j, 0).start()
 
-    for k in range(max(nz + 2, near + 1)):
-        if 1 <= k < nz + 2:
-            gather_slot(0, k, 0)
+    each = -(-(p.S - 1) // near)
+    for k in range(near + 1):
         if k < near:
+            for n in range(1 + k * each, min(1 + (k + 1) * each, p.S)):
+                part = wcol.at[:, q_rows(q_from(n), here.side), :]
+                remote(part, part, q_ss.at[n], q_rs.at[q_from(n)], s, here.r).wait_recv()
+                q_twin(q_from(n), here.side).start()
             a_at(k, a_near)
-        if 1 <= k < near + 1:
+        if k == START:
+            for w in range(nw):
+                gather_rows(w)
+        if k >= 1:
             a_at(k - 1, a_far)
-        if k == near - 1:
-            for w in range(1, nw):
-                gather_start(w)
+        if k >= near + 1 - EARLY:
+            for w in range(nw):
+                gather_slot(w, k - (near - EARLY), LAG)
 
     @pl.when(jnp.logical_not(primary))
     def _():
@@ -432,17 +469,9 @@
     row = here.um * p.Q + here.uq
     preu[...] = jnp.broadcast_to(pre2[pl.ds(row, 1), :], preu.shape)
 
-    gather_wait(0)
-    local[0].wait()
-    cols = []
-    for h in range(p.pairs):
-        for k in range(3):
-            start = pl.multiple_of(k * p.D + here.group * p.W + h * PAIR, PAIR)
-            src = wqf.at[:, pl.ds(start, PAIR)]
-            cols.append(pltpu.make_async_copy(src, wcol.at[h, :, pl.ds(k * PAIR, PAIR)], col_sem.at[h, k]))
-            cols[-1].start()
-    for copy in cols:
-        copy.wait()
+    for n in range(1, p.S):
+        q_twin(q_from(n), 1 - here.side).wait_recv()
+    q_own.wait()
     own = pl.ds(pl.multiple_of(here.group * p.W, PAIR), p.W)
     q_bias = parf[0:1, own].astype(F32)
     v_bias = parf[1:2, own].astype(F32)
@@ -461,7 +490,7 @@
     lax.fori_loop(0, p.nq, project, 0)
 
     prefix = preu[0:1, 0:1]
-    slots = nz + 1 + LAG
+    slots = nz + 1 + LAG - EARLY
     per = -(-slots // p.nq)
 
     def o_copy(i):
@@ -503,8 +532,8 @@
         launch(*o_copy(i))
 
         for extra in range(per):
-            for w in range(1, nw):
-                gather_slot(w, i * per + extra + 1, LAG)
+            for w in range(nw):
+                gather_slot(w, i * per + extra + 1 + EARLY, LAG)
 
         return carry
 
@@ -525,8 +554,11 @@
     for copy in small:
         copy.wait_send()
     swap.wait_send()
-    for copy in local[1:]:
+    for copy in local:
         copy.wait()
+    for n in range(1, p.S):
+        q_send(n).wait_send()
+        q_twin(q_from(n), here.side).wait_send()
     for m in range(p.M):
         to, far = first_hop(m)
 
@@ -543,12 +575,11 @@
                 a_forward(jj * p.cpu + lax.rem(here.lane + k, p.cpu), 0).wait_send()
 
     for w in range(nw):
-        if w:
-            gather_wait(w)
+        gather_wait(w)
         gather_drain(w)
 
 
-def fore(plan, x, par, pre, weights):
+def fore(plan, x, par, pre, qkv, weights):
     p = plan
     nz = p.S // 2
     nw = len(weights)
@@ -566,7 +597,7 @@
     return pl.pallas_call(
         functools.partial(fore_kernel, p),
         out_shape=out_shape,
-        in_specs=[vmem] * (3 + nw),
+        in_specs=[vmem] * (4 + nw),
         out_specs=[any_space] * nw + [vmem] * 11,
         scratch_shapes=[
             pltpu.VMEM((p.S,) + par.shape, BF16),
@@ -575,13 +606,14 @@
             dma((p.M,)), dma((p.P,)), dma((p.P, p.cpu)),
             dma((nw, 2, nz)), dma((nw, 2, nz)), dma((nw, nz)), dma((nw, nz)),
             dma((nw, 2, nz)), dma((nw, 2, nz)), dma((nw, 4, nz)), dma((nw, 4, nz)),
-            dma((p.nq,)), dma((p.M, p.groups, p.pieces)), dma((p.pairs, 3)),
+            dma((p.nq,)), dma((p.M, p.groups, p.pieces)),
+            dma((p.S,)), dma((p.S,)), dma((p.S,)), dma((p.S,)), dma((1,)),
         ],
         compiler_params=pltpu.CompilerParams(
             collective_id=0, has_side_effects=True, vmem_limit_bytes=VMEM_LIMIT
         ),
         name="fore",
-    )(x, par, pre, *weights)
+    )(x, par, pre, qkv, *weights)
 
 
 class GridSum:
@@ -707,11 +739,16 @@
         def _():
             self.final(w, k).start()
 
-    def events(self):
-        return self.nw * self.nz + 2 * SUM_LAG
+    def slots(self):
+        return CADENCE * (self.nw * self.nz + 2 * SUM_LAG)
+
+    def slot(self, n):
+        @pl.when(lax.rem(n, CADENCE) == 0)
+        def _():
+            self.event(n // CADENCE)
 
     def event(self, n):
-        for stage, body in enumerate((self.event_one, self.event_two, self.event_three)):
+        for stage, body in ((2, self.event_three), (1, self.event_two), (0, self.event_one)):
             e = n - stage * SUM_LAG
             for w in range(self.nw):
                 ok = jnp.logical_and(e >= 0, e < self.nw * self.nz)
@@ -812,7 +849,6 @@
     (do_ss, do_rs, dm_s, dm_r, dy_s, dy_r, dh_s, dh_r, wt_s, wt_r, wz_s, wz_r, wx_s, wx_r, wd_s, wd_r) = rest[17:33]
     (ss_s, ss_r, sa_s, sa_r) = rest[33:37]
     sums = GridSum(here, grads, outs, rest[37:])
-    per = -(-sums.events() // (p.pairs * p.nq))
     greet(sum_peers(here))
     rows_here = pl.ds(pl.multiple_of(lax.rem(s, p.P) * p.T, p.T), p.T)
 
@@ -841,7 +877,7 @@
             a_all.at[:, pl.ds(pl.multiple_of(b * BQ, BQ), BQ)], a_buf.at[slot], a_sem.at[slot]
         )
 
-    def weight_part(h, dst):
+    def weight_part(h, dst, slot_from=None):
         def some(b, carry):
             slot = lax.rem(b, 2)
 
@@ -851,6 +887,8 @@
 
             a_load(b).wait()
             dst[pl.ds(pl.multiple_of(b * BQ, BQ), BQ), :] = dot(a_buf[slot], low[h], 0, 0).astype(BF16)
+            if slot_from is not None:
+                sums.slot(slot_from + b)
             return carry
 
         lax.fori_loop(0, p.D // BQ, some, 0)
@@ -873,12 +911,13 @@
         dk_acc[...] = jnp.zeros_like(dk_acc)
         dv_acc[...] = jnp.zeros_like(dv_acc)
 
-        def query_step(i, inner):
+        def query_step(n, inner):
+            j = lax.rem((here.unit - here.uq * near) * p.cpu + n // p.pieces, p.P)
+            i = j * p.pieces + lax.rem(n, p.pieces)
             rows = block_rows(i)
 
-            @pl.when(jnp.logical_and(turn == 0, lax.rem(i, p.pieces) == 0))
+            @pl.when(jnp.logical_and(turn == 0, lax.rem(n, p.pieces) == 0))
             def _():
-                j = i // p.pieces
                 part = do_all.at[pl.ds(pl.multiple_of(j * p.T, p.T), p.T), :]
                 pltpu.make_async_copy(part, part, do_rs.at[j]).wait()
 
@@ -906,8 +945,7 @@
                     total = total + dot(k_turn[e * HEAD : (e + 1) * HEAD, keys], dlog)
                 dq_t.append(total)
             low[h, rows, 0:PAIR] = (jnp.concatenate(dq_t, axis=0).T * SCALE).astype(BF16)
-            for extra in range(per):
-                sums.event((turn * p.nq + i) * per + extra)
+            sums.slot(turn * p.nq + n)
             return inner
 
         lax.fori_loop(0, p.nq, query_step, 0)
@@ -944,18 +982,45 @@
         rows = block_rows(i)
         return remote(da_out.at[rows, :], da_in.at[rows, :], dm_s.at[n], dm_r.at[i], s, here.mate)
 
+    far_blocks = (p.cpu - 1) * near * p.pieces
+    count = p.pairs * p.nq
+
+    def side_rows(i):
+        return block_rows((i // p.pieces // p.cpu) * p.pieces + lax.rem(i, p.pieces))
+
+    def da_over(n, i):
+        return remote(da_own.at[block_rows(i), :], da_side.at[side_rows(i), :], dy_s.at[n], dy_r.at[i], here.beside, here.r)
+
     def da_first(n, carry):
-        i = block_of(n)
-        rows = block_rows(i)
-        da_out[rows, :] = da_half(rows, 1 - c).astype(BF16)
-        da_mate(n, i).start()
-        da_own[rows, :] = da_half(rows, c).astype(BF16)
+        @pl.when(n < p.nq)
+        def _():
+            i = block_of(n)
+            rows = block_rows(i)
+            da_out[rows, :] = da_half(rows, 1 - c).astype(BF16)
+            da_mate(n, i).start()
+            da_own[rows, :] = da_half(rows, c).astype(BF16)
+
+        @pl.when(n > 0)
+        def _():
+            last = jnp.maximum(n - 1, 0)
+            i = block_of(last)
+            rows = block_rows(i)
+            da_mate(last, i).wait_recv()
+            da_own[rows, :] = (da_own[rows, :].astype(F32) + da_in[rows, :].astype(F32)).astype(BF16)
+
+            @pl.when(last < far_blocks)
+            def _():
+                da_over(last, i).start()
+
+        sums.slot(count + n)
         return carry
 
-    lax.fori_loop(0, p.nq, da_first, 0)
+    lax.fori_loop(0, p.nq + 1, da_first, 0)
+    count = count + p.nq + 1
 
     own_pair = here.side
-    weight_part(own_pair, dw_own)
+    weight_part(own_pair, dw_own, count)
+    count = count + p.D // BQ
     to_twin_dw().wait_recv()
     dw_own[...] = (dw_own[...].astype(F32) + dw_in[...].astype(F32)).astype(BF16)
     span = 2 * width
@@ -971,14 +1036,6 @@
 
     for n in range(nz - 1):
         dw_send(n).start()
-
-    far_blocks = (p.cpu - 1) * near * p.pieces
-
-    def side_rows(i):
-        return block_rows((i // p.pieces // p.cpu) * p.pieces + lax.rem(i, p.pieces))
-
-    def da_over(n, i):
-        return remote(da_own.at[block_rows(i), :], da_side.at[side_rows(i), :], dy_s.at[n], dy_r.at[i], here.beside, here.r)
 
     def da_back(n, i):
         rows = block_rows(i)
@@ -993,23 +1050,20 @@
     def da_second(n, carry):
         i = block_of(n)
         rows = block_rows(i)
-        da_mate(n, i).wait_recv()
-        pair = da_own[rows, :].astype(F32) + da_in[rows, :].astype(F32)
-
-        @pl.when(n < far_blocks)
-        def _():
-            da_own[rows, :] = pair.astype(BF16)
-            da_over(n, i).start()
-
-        @pl.when(n >= far_blocks)
-        def _():
-            da_over(n, i).wait_recv()
-            da_own[rows, :] = (pair + da_side[side_rows(i), :].astype(F32)).astype(BF16)
-            launch(*da_back(n, i))
-
+        da_over(n, i).wait_recv()
+        da_own[rows, :] = (da_own[rows, :].astype(F32) + da_side[side_rows(i), :].astype(F32)).astype(BF16)
+        launch(*da_back(n, i))
+        sums.slot(count + n - far_blocks)
         return carry
 
-    lax.fori_loop(0, p.nq, da_second, 0)
+    lax.fori_loop(far_blocks, p.nq, da_second, 0)
+    count = count + p.nq - far_blocks
+
+    def rest_of_sums(n, carry):
+        sums.slot(n)
+        return carry
+
+    lax.fori_loop(count, max(count, sums.slots()), rest_of_sums, 0)
     sums.finish()
 
     dw_far[here.row] = dw_own[dw_rows(here.row), :]
@@ -1222,10 +1276,12 @@
     spare = max(128 - width, 0)
     par = jnp.concatenate([qv_bias, branch_bias, norm_gain, norm_bias, up_bias.reshape(-1, width)], axis=0)
     par = jnp.pad(par, ((0, 0), (0, spare)))
+    by_group = qkv_weight.reshape(-1, 3, p.groups, p.pairs, PAIR).transpose(2, 3, 0, 1, 4)
+    by_group = by_group.reshape(p.groups, p.pairs, -1, 3 * PAIR)
     pre = jnp.broadcast_to(prefix[:, 0].reshape(-1, 1).astype(F32), (p.M * p.Q, 128))
     pre = jnp.pad(pre, ((0, 8 - p.M * p.Q), (0, 0)))
-    (_, wo, wu, wd, parf, _, q, k, v, o, lse, preu, o_home, a_unit, w_unit) = fore(
-        p, x, par, pre, (qkv_weight, out_weight, up_weight, down_weight)
+    (wo, wu, wd, parf, _, q, k, v, o, lse, preu, o_home, a_unit, w_unit) = fore(
+        p, x, par, pre, by_group, (out_weight, up_weight, down_weight)
     )
     par32 = parf.astype(F32)
     bias_branch = par32[2:4]

time: 476 us -> 439 us (0.922)
  the two profiles are of different devices: /device:TPU:25 before, /device:TPU:0 now
where the time goes in v3:
time: 439 us; the launch traced here: 436 us
  Pallas kernels  340 us (77%)
  matrix products  63 us (14%)
  local copies, waits for them, and re-layouts  18.2 us (4%)
  other arithmetic  13.2 us (3%)
    pallas_call x1, Pallas kernels, back(): pl.pallas_call(functools.partial(back_kernel, p, nw), out_shape=[shape((p...  185 us
    pallas_call x1, Pallas kernels, fore(): pl.pallas_call(functools.partial(fore_kernel, p), out_shape=out_shape, in...  155 us
    dot_general x9, matrix products, dot(): lax.dot_general(a, b, (((ca,), (cb,)), ((), ())), preferred_element_type=...  63 us

profile of v3, /device:TPU:0, one launch (start us, length us, event | category | flops | bytes accessed | tf_op | source)
XLA Modules:
  0.0 436.0 jit_solution(1564762803421127453)
XLA Ops:
  0.6 2.6 concatenate.26.par
  4.6 1.5 copy.32
  6.2 1.2 copy.34.wq
  7.3 155.4 %fore.1 = (bf16[1024,1024]{1,0:T(8,128)(2,1)}, bf16[1024,4096]{1,0:T(8,128)(2,1)}, bf16[4096,1024]{1,0:T(8,128)(2,1)}, bf16[16,1024]{1,0:T(8,128)(2,1)}, bf16[2,...) custom-call(bf16[2,256,1024]{2,1,0:T(8,128)(2,1)} %bitcast.97, ...), custom_call_target="tpu_custom_call" | custom-call | tf_op jit(solution)/shard_map/fore/pallas_call | solution.py:597
  162.7 0.9 fusion.16
  163.6 0.7 slice.72
  164.3 3.4 add_reduce_fusion.1
  168.2 0.8 copy-done.2
  169.0 0.8 fusion.15
  170.2 11.5 %fusion.3 = (f32[512,4096]{1,0:T(8,128)}, bf16[512,4096]{1,0:T(8,128)(2,1)}) fusion(f32[4096]{0:T(1024)S(1)} %bitcast.132, bf16[1024,4096]{1,0:T(8,128)(2,1)S(1)} %bitcast.144, f32[512,1024]{1,0:T(8,128)S(1)} %get-tuple-element.106, f32[1024]{0:T(1024)S(1)} %bitcast.138, f32[1024]{0:T(1024)S(1)} %bitcast.134, f32[512]{0:T(512)S(1)} %fusion.9, ...), kind=kOutput, calls=%fused_computation.4 | convolution fusion | flops 4320657408 | bytes 23097344 | tf_op jit(solution)/shard_map/dot_general | solution.py:136
  181.8 6.8 %add_reduce_fusion = (f32[512]{0:T(512)S(1)}, f32[512,1024]{1,0:T(8,128)S(1)}) fusion(f32[1024]{0:T(1024)S(1)} %bitcast.118, bf16[512,4096]{1,0:T(8,128)(2,1)} %get-tuple-element.36, bf16[4096,1024]{1,0:T(8,128)(2,1)S(1)} %bitcast.146), kind=kOutput, calls=%fused_computation.37 | convolution fusion | flops 4296015360 | bytes 14686208 | tf_op jit(solution)/shard_map/dot_general | solution.py:136
  189.0 0.8 copy-done.1
  189.8 0.9 fusion.7
  190.8 2.1 fusion.14
  193.1 10.9 %convert_reduce_fusion = (f32[4096]{0:T(1024)S(1)}, bf16[512,4096]{1,0:T(8,128)(2,1)}) fusion(f32[512,4096]{1,0:T(8,128)} %get-tuple-element.44, bf16[512,1024]{1,0:T(8,128)(2,1)S(1)} %get-tuple-element.95, bf16[4096,1024]{1,0:T(8,128)(2,1)} %get-tuple-element.37), kind=kOutput, calls=%fused_computation.5 | convolution fusion | flops 4303351808 | bytes 22036480 | tf_op jit(solution)/shard_map/dot_general | solution.py:136
  204.0 8.7 %multiply_reduce_fusion = (f32[1024]{0:T(1024)S(1)}, f32[512]{0:T(512)S(1)}, f32[1024]{0:T(1024)S(1)}, f32[512,1024]{1,0:T(8,128)S(1)}) fusion(f32[512,1024]{1,0:T(8,128)S(1)} %get-tuple-element.106, f32[512]{0:T(512)S(1)} %fusion.9, f32[512]{0:T(512)S(1)} %broadcast_multiply_fusion.1, f32[1024]{0:T(1024)S(1)} %bitcast.135, ...), kind=kOutput, calls=%fused_computation.23 | convolution fusion | flops 4299159040 | bytes 16795648 | tf_op jit(solution)/shard_map/dot_general | solution.py:136
  212.8 0.7 fusion.13
  213.5 1.2 multiply_reduce_fusion.1
  214.7 0.8 fusion.12
  216.3 1.7 copy-done.10
  218.0 2.3 convolution_convert_fusion.3
  220.5 1.3 concatenate.36
  221.8 9.4 %convolution_convert_fusion.1 = bf16[4096,1024]{1,0:T(8,128)(2,1)} fusion(bf16[512,4096]{1,0:T(8,128)(2,1)} %get-tuple-element.36, bf16[512,1024]{1,0:T(8,128)(2,1)S(1)} %get-tuple-element.95), kind=kOutput, calls=%fused_computation.10 | convolution fusion | flops 4299161600 | bytes 13631488 | tf_op jit(solution)/shard_map/dot_general | solution.py:136
  231.2 7.3 %convolution_convert_fusion = bf16[1024,4096]{1,0:T(8,128)(2,1)} fusion(bf16[512,4096]{1,0:T(8,128)(2,1)S(1)} %copy-done.12, f32[512,1024]{1,0:T(8,128)S(1)} %get-tuple-element.106, f32[1024]{0:T(1024)S(1)} %bitcast.139, f32[1024]{0:T(1024)S(1)} %bitcast.137, f32[512]{0:T(512)S(1)} %fusion.9, f32[512]{0:T(512)S(1)} %broadcast_multiply_fusion.1), kind=kOutput, calls=%fused_computation.9 | convolution fusion | flops 4301783040 | bytes 14692352 | tf_op jit(solution)/shard_map/dot_general | solution.py:136
  238.5 2.6 convolution_convert_fusion.2
  241.2 185.1 %back.1 = (bf16[2,256,1024]{2,1,0:T(8,128)(2,1)}, bf16[8,128,384]{2,1,0:T(8,128)(2,1)}, f32[16,128]{1,0:T(8,128)}, bf16[2,256,1024]{2,1,0:T(8,128)(2,1)}, bf16[2...) custom-call(bf16[2048,256]{1,0:T(8,128)(2,1)} %get-tuple-element.38.refs_0_, ...), custom_call_target="tpu_custom_call" | custom-call | tf_op jit(solution)/shard_map/back/pallas_call | solution.py:1211
  426.3 1.4 copy.36
  427.9 1.6 copy.40
  430.1 0.9 bitcast_convert_fusion.2
  430.9 1.6 bitcast_convert_fusion.1
  433.1 1.6 bitcast_convert_fusion
  434.8 1.0 copy.42
  (60 shorter events, 5.2 us)
Async XLA Ops:
  164.3 5.8 %slice-start = ((s8[8388608]{0:T(1024)(128)(4,1)}), s8[4194304]{0:T(1024)(128)(4,1)S(1)}, s32[]{:S(2)}) async-start(s8[8388608]{0:T(1024)(128)(4,1)} %bitcast.143), calls=%async_computation | async-start | bytes 8388608
  167.7 1.2 copy-start.2
  167.8 2.5 slice-start.1
  169.8 12.0 %slice-start.2 = ((s8[8388608]{0:T(1024)(128)(4,1)}), s8[4194304]{0:T(1024)(128)(4,1)S(1)}, s32[]{:S(2)}) async-start(s8[8388608]{0:T(1024)(128)(4,1)} %bitcast.145), calls=%async_computation.2 | async-start | bytes 8388608
  170.2 11.5 %slice-start.3 = ((s8[8388608]{0:T(1024)(128)(4,1)}), s8[4194304]{0:T(1024)(128)(4,1)S(1)}, s32[]{:S(2)}) async-start(s8[8388608]{0:T(1024)(128)(4,1)} %bitcast.145), calls=%async_computation.3 | async-start | bytes 8388608
  188.6 1.2 copy-start.1
  214.7 1.3 copy-start
  216.0 2.0 copy-start.10
  216.3 4.0 copy-start.5
  221.8 9.4 %copy-start.12 = (bf16[512,4096]{1,0:T(8,128)(2,1)S(1)}, bf16[512,4096]{1,0:T(8,128)(2,1)}, u32[]{:S(2)}) copy-start(bf16[512,4096]{1,0:T(8,128)(2,1)} %get-tuple-element.129) | copy-start | bytes 12582916
  231.2 7.3 %copy-start.6 = (bf16[512,1024]{1,0:T(8,128)(2,1)S(1)}, bf16[512,1024]{1,0:T(8,128)(2,1)}, u32[]{:S(2)}) copy-start(bf16[512,1024]{1,0:T(8,128)(2,1)} %copy-done.5) | copy-start | bytes 3145732
  231.2 7.3 %copy-start.11 = (bf16[2,256,1024]{2,1,0:T(8,128)(2,1)S(1)}, bf16[2,256,1024]{2,1,0:T(8,128)(2,1)}, u32[]{:S(2)}) copy-start(bf16[2,256,1024]{2,1,0:T(8,128)(2,1)} %get-tuple-element.32) | copy-start | bytes 3145732
  427.8 1.6 copy-start.9
  427.9 2.2 copy-start.8
  427.9 3.1 copy-start.4
  429.5 3.6 copy-start.3
  432.5 2.2 copy-start.7
